TPU v7x, 32 devices: a whole 2x2x4 slice. The times are simulated.
32 devices in a mesh: gx: 8 (over z, core), gy: 4 (over y, x).
Axes of the slice: x: 2, y: 2, z: 4, core: 2. Of those that a mesh axis runs over, the one named last changes fastest.
Arguments:
- grid_field: bfloat16 [1, 20, 2048, 2048], P(None, None, 'gx', 'gy'), may hold values from -8 to 8
- spectral_weight: float32 [2, 2, 20, 20, 2048], P(None, None, None, None, ('gx', 'gy')), may hold values from -1 to 1
- conv_near: bfloat16 [2, 20, 180], replicated, may hold values from -0.4375 to 0.4375
- conv_far: bfloat16 [2, 20, 500], replicated, may hold values from -0.25 to 0.25
- mix_logits: float32 [2, 3], replicated, may hold values from -1 to 1
- channel_bias: float32 [2, 20], replicated, may hold values from -3 to 3
Outputs:
- result_field: bfloat16 [1, 20, 2048, 2048], P(None, None, 'gx', 'gy')
All inputs are finite; a program needn't handle non-finite values.
Results may differ from a plain program's by a relative error of at most 0.004.
Values may be sent and summed in bfloat16 or wider, within the bound.
A program may use at most 448 MiB of HBM per device.

v0:
```python
import functools
import math

import jax
import jax.numpy as jnp
from jax import lax
from jax.experimental import pallas as pl
from jax.experimental.pallas import tpu as pltpu
from jax.sharding import PartitionSpec as P

full_turn = 2.0 * math.pi
MESH = pl.DeviceIdType.MESH
MODES_Y = 32
GROUP = 16
LANES = 128
NEAR = (-1, 0, 1)
FAR = (-4, -2, 0, 2, 4)
f32 = jnp.float32
bf16 = jnp.bfloat16


def split_bf16(value):
    high = value.astype(bf16)
    low = (value - high.astype(f32)).astype(bf16)
    return high, low


def prep_kernel(near_ref, far_ref, near_out, far_out):
    channels = near_ref.shape[1]
    pair = 2 * channels
    rows, depth = 4 * pair, 6 * pair

    def spread(taps_ref, out_ref, side, tap_of):
        taps = taps_ref[0]
        count = taps.shape[1]
        replicate = (
            lax.broadcasted_iota(jnp.int32, (rows, channels), 0) % channels
            == lax.broadcasted_iota(jnp.int32, (rows, channels), 1)
        ).astype(bf16)
        tall = jnp.dot(replicate, taps, preferred_element_type=f32).astype(bf16)
        source = lax.broadcasted_iota(jnp.int32, (count, depth), 0)
        target = lax.broadcasted_iota(jnp.int32, (count, depth), 1)
        same = source % channels == target % channels
        tap = source // channels
        out_at = lax.broadcasted_iota(jnp.int32, (rows, depth), 0)
        in_at = lax.broadcasted_iota(jnp.int32, (rows, depth), 1)
        wanted = tap_of(out_at // channels, in_at // channels)
        pieces = []
        for column in range(side):
            total = jnp.zeros((rows, depth), f32)
            for row in range(side):
                pick = (same & (tap == row * side + column)).astype(bf16)
                term = jnp.dot(tall, pick, preferred_element_type=f32)
                total = jnp.where(wanted == row, term, total)
            pieces.append(total)
        out_ref[0] = jnp.concatenate(pieces, axis=1).astype(bf16)

    def far_tap(out_row, in_row):
        return in_row - out_row

    def near_tap(out_row, in_row):
        out_pair, out_low = out_row // 2, out_row % 2
        out_at = 4 * (out_pair % 2) + 2 * out_low + out_pair // 2
        in_pair, in_low = in_row // 2, in_row % 2
        odd = 4 * (in_pair // 2 - 1) + 1 + 2 * in_low
        even = 4 * (in_pair // 2) + 2 * in_low
        in_at = jnp.where(in_pair % 2 == 0, odd, even)
        return in_at - out_at + 1

    spread(near_ref, near_out, 3, near_tap)
    spread(far_ref, far_out, 5, far_tap)


def prep_call(near, far):
    layers, channels, _ = near.shape
    rows, depth = 8 * channels, 12 * channels
    block = lambda shape: pl.BlockSpec((1,) + shape[1:], lambda i: (i, 0, 0))
    near_shape = (layers, rows, 3 * depth)
    far_shape = (layers, rows, 5 * depth)
    return pl.pallas_call(
        prep_kernel,
        grid=(layers,),
        name="prep",
        in_specs=[block(near.shape), block(far.shape)],
        out_specs=[block(near_shape), block(far_shape)],
        out_shape=[
            jax.ShapeDtypeStruct(near_shape, bf16),
            jax.ShapeDtypeStruct(far_shape, bf16),
        ],
    )(near, far)


def main_kernel(
    u_ref, sw_ref, near_ref, far_ref, order_ref, back_ref, fwd_ref, ftab_ref, itab_ref, inv_ref,
    bias_ref, mix_ref, out_ref,
    nst, fst, conv, lhs, lines, carry, pack, packs, edges, hcol, hrow,
    sendbuf, recv, mixed, gath,
    halo_send, halo_recv, a2a_send, a2a_recv, gat_send, gat_recv,
    *, sizes, first_part,
):
    gx, gy = sizes
    devices = gx * gy
    layers = sw_ref.shape[0]
    channels, local_rows, cols = u_ref.shape
    pair = 2 * channels
    half = 4 * pair
    whole = 2 * half
    groups = local_rows // GROUP
    wide = cols + 2 * LANES
    slot = mixed.shape[1]
    blocks = sendbuf.shape[1] // slot
    sharers = devices // blocks
    per_device = 2 * MODES_Y
    my_x, my_y = lax.axis_index("gx"), lax.axis_index("gy")
    me = my_x * gy + my_y

    def place(index):
        return (index // gy, index % gy)

    barrier = pltpu.get_barrier_semaphore()

    @pl.loop(1, devices)
    def _(k):
        pl.semaphore_signal(
            barrier, inc=1, device_id=place((me + k) % devices), device_id_type=MESH
        )

    def store_rows(g, even, odd, start):
        width = even.shape[1]
        at = slice(start, start + width)
        old_even, old_odd = carry[0, :, at], carry[1, :, at]
        q = [(even[i * pair : (i + 1) * pair], odd[i * pair : (i + 1) * pair]) for i in range(4)]
        near_rows = [old_odd]
        for i in range(4):
            near_rows.append(q[i][0])
            if i < 3:
                near_rows.append(q[i][1])
        nst[pl.ds(pl.multiple_of(g * whole, whole), whole), at] = jnp.concatenate(
            near_rows, axis=0
        ).astype(bf16)
        row = pl.ds(pl.multiple_of(g * half, half), half)
        fst[0, row, at] = jnp.concatenate([old_even, even[: 3 * pair]], axis=0).astype(bf16)
        fst[1, row, at] = jnp.concatenate([old_odd, odd[: 3 * pair]], axis=0).astype(bf16)
        carry[0, :, at] = q[3][0]
        carry[1, :, at] = q[3][1]

    lane = lax.broadcasted_iota(jnp.int32, (half, LANES), 1)

    def ingest(g, value, layer):
        even, odd = value[:half], value[half:]
        store_rows(g, even, odd, LANES)
        lines[pl.ds(pl.multiple_of(g * whole, whole), whole), :] = jnp.dot(
            value.astype(bf16), fwd_ref[...], preferred_element_type=f32
        )
        for p, part in enumerate((even, odd)):
            k = 2 * g + p
            mine = lane // 4 == k
            left = pltpu.roll(part[:, :LANES], 4 * k, 1)
            right = pltpu.roll(part[:, cols - LANES :], (4 * k + 4) % LANES, 1)
            pack[0] = jnp.where(mine, left, pack[0])
            pack[1] = jnp.where(mine, right, pack[1])

        @pl.when(g == 0)
        def _():
            edges[layer, 0] = jnp.concatenate([even[:pair], odd[:pair]], axis=0).astype(bf16)

        @pl.when(g == groups - 1)
        def _():
            edges[layer, 1] = jnp.concatenate(
                [even[3 * pair :], odd[3 * pair :]], axis=0
            ).astype(bf16)

    carry[...] = jnp.zeros_like(carry)
    pack[...] = jnp.zeros_like(pack)

    @pl.loop(0, groups)
    def _(g):
        slab = u_ref[:, pl.ds(pl.multiple_of(g * GROUP, GROUP), GROUP), :]
        value = jnp.dot(
            order_ref[...], slab.reshape(whole, cols), preferred_element_type=f32
        )
        ingest(g, value, 0)

    pl.semaphore_wait(barrier, devices - 1)

    up, down = (my_x + gx - 1) % gx, (my_x + 1) % gx
    left, right = (my_y + gy - 1) % gy, (my_y + 1) % gy
    last = cols - LANES

    def halo_copies(layer):
        def copy(i, src, dst, target):
            return pltpu.make_async_remote_copy(
                src_ref=src, dst_ref=dst, send_sem=halo_send.at[layer, i],
                recv_sem=halo_recv.at[layer, i], device_id=target, device_id_type=MESH,
            )

        top, bottom = edges.at[layer, 0], edges.at[layer, 1]
        above, below = hrow.at[layer, 0], hrow.at[layer, 1]
        head, mid, tail = slice(0, LANES), slice(LANES, LANES + cols), slice(LANES + cols, wide)
        return [
            copy(0, packs.at[layer, 0], hcol.at[layer, 1], (my_x, left)),
            copy(1, packs.at[layer, 1], hcol.at[layer, 0], (my_x, right)),
            copy(2, top, below.at[:, mid], (up, my_y)),
            copy(3, bottom, above.at[:, mid], (down, my_y)),
            copy(4, top.at[:, :LANES], below.at[:, tail], (up, left)),
            copy(5, bottom.at[:, :LANES], above.at[:, tail], (down, left)),
            copy(6, top.at[:, last:], below.at[:, head], (up, right)),
            copy(7, bottom.at[:, last:], above.at[:, head], (down, right)),
        ]

    def a2a_copy(layer, k):
        target = (me + k) % devices
        return pltpu.make_async_remote_copy(
            src_ref=sendbuf.at[layer, pl.ds(target // sharers * slot, slot)],
            dst_ref=recv.at[layer, k - 1],
            send_sem=a2a_send.at[layer, k - 1],
            recv_sem=a2a_recv.at[layer, k - 1],
            device_id=place(target),
            device_id_type=MESH,
        )

    def gather_copy(layer, k):
        return pltpu.make_async_remote_copy(
            src_ref=mixed.at[layer],
            dst_ref=gath.at[layer, pl.ds(me * slot, slot)],
            send_sem=gat_send.at[layer, k - 1],
            recv_sem=gat_recv.at[layer, k - 1],
            device_id=place((me + k) % devices),
            device_id_type=MESH,
        )

    modes_x = ftab_ref.shape[0] // 2
    share_rows = modes_x // blocks
    share = sw_ref.shape[-1]

    def turned(value):
        at = lax.broadcasted_iota(jnp.int32, value.shape, 1)
        return jnp.where(
            (at // MODES_Y) % 2 == 1,
            pltpu.roll(value, MODES_Y, 1),
            -pltpu.roll(value, LANES - MODES_Y, 1),
        )

    def row_transform(layer):
        @pl.loop(0, channels)
        def _(c):
            high, low = split_bf16(lines[pl.ds(c, local_rows, stride=channels), :])
            both = jnp.dot(
                ftab_ref[...],
                jnp.concatenate([high, low, high], axis=0),
                preferred_element_type=f32,
            )
            total = both[:modes_x] + pltpu.roll(both[modes_x:], per_device, 1)
            if share_rows == 2:
                at = lax.broadcasted_iota(jnp.int32, (blocks, LANES), 1)
                block = jnp.where(
                    at < per_device, total[:blocks], pltpu.roll(total[blocks:], per_device, 1)
                )
            else:
                block = total
            sendbuf[layer, pl.ds(c, blocks, stride=slot), :] = block

    def mix_modes(layer):
        own = sendbuf[layer, pl.ds(pl.multiple_of(me // sharers * slot, 8), slot), :]

        @pl.loop(1, devices)
        def _(k):
            a2a_copy(layer, k).wait_recv()

        own = own + jnp.sum(recv[layer], axis=0)
        crossed = turned(own)
        scale = mix_ref[layer, 0]

        def spread(part):
            if share_rows == 1:
                tiled = jnp.concatenate([part] * (LANES // share), axis=1)
                at = lax.broadcasted_iota(jnp.int32, tiled.shape, 1) // share
                return jnp.where(at % sharers == me % sharers, tiled, 0.0)
            pieces = []
            for j in range(share_rows):
                piece = part[:, j * MODES_Y : (j + 1) * MODES_Y]
                pieces += [piece, piece]
            return jnp.concatenate(pieces, axis=1)

        total = jnp.zeros((channels, LANES), f32)
        for c in range(channels):
            total = total + spread(sw_ref[layer, 0, c]) * own[c : c + 1]
            total = total + spread(sw_ref[layer, 1, c]) * crossed[c : c + 1]
        total = total * scale
        mixed[layer, :channels, :] = total
        gath[layer, pl.ds(pl.multiple_of(me * slot, 8), channels), :] = total

        @pl.loop(1, devices)
        def _(k):
            gather_copy(layer, k).start()

    def inverse_rows(layer):
        @pl.loop(1, devices)
        def _(k):
            gather_copy(layer, k).wait_recv()

        @pl.loop(0, channels)
        def _(o):
            block = gath[layer, pl.ds(o, blocks, stride=slot * sharers), :]
            for i in range(1, sharers):
                block = block + gath[layer, pl.ds(i * slot + o, blocks, stride=slot * sharers), :]
            cross = turned(block)
            if share_rows == 2:
                stack = [block, pltpu.roll(block, per_device, 1)]
                stack += [cross, pltpu.roll(cross, per_device, 1)]
            else:
                stack = [block, cross]
            high, low = split_bf16(jnp.concatenate(stack, axis=0))
            lhs[pl.ds(o, local_rows, stride=channels), :] = jnp.dot(
                itab_ref[...],
                jnp.concatenate([high, low, high], axis=0),
                preferred_element_type=f32,
            )

    def conv_group(layer, g):
        near_w, far_w = near_ref[layer], far_ref[layer]
        depth = 6 * pair

        def window(rows, shifts):
            return jnp.concatenate([rows[:, LANES + d : LANES + d + cols] for d in shifts], axis=0)

        near = []
        for h in range(2):
            rows = nst[pl.ds(pl.multiple_of(g * whole, whole) + h * half, depth), :]
            near.append(jnp.dot(near_w, window(rows, NEAR), preferred_element_type=f32))
        parts = []
        for p in range(2):
            rows = fst[p, pl.ds(pl.multiple_of(g * half, half), depth), :]
            far = jnp.dot(far_w, window(rows, FAR), preferred_element_type=f32)
            side = slice(p * 2 * pair, (p + 1) * 2 * pair)
            close = jnp.concatenate([near[0][side], near[1][side]], axis=0)
            total = mix_ref[layer, 1] * close + mix_ref[layer, 2] * far + bias_ref[layer]
            parts.append(total)
        conv[pl.ds(pl.multiple_of(g * whole, whole), whole), :] = jnp.concatenate(parts, axis=0)

    def finish_group(layer, g):
        at = pl.ds(pl.multiple_of(g * whole, whole), whole)
        high, low = split_bf16(lhs[at, :per_device])
        spectral = jnp.dot(
            jnp.concatenate([high, low, high], axis=1), inv_ref[...], preferred_element_type=f32
        )
        value = conv[at, :] + spectral
        value = (value * 0.5 * (1.0 + lax.erf(value * (0.5**0.5)))).astype(bf16)
        if layer + 1 < layers:
            ingest(g, value.astype(f32), layer + 1)
        else:
            natural = jnp.dot(back_ref[...], value, preferred_element_type=f32).astype(bf16)
            out_ref[:, pl.ds(pl.multiple_of(g * GROUP, GROUP), GROUP), :] = natural.reshape(
                channels, GROUP, cols
            )

    for layer in range(layers):
        packs[layer] = pack[...].astype(bf16)
        halos = halo_copies(layer)
        for copy in halos:
            copy.start()
        row_transform(layer)

        @pl.loop(1, devices)
        def _(k):
            a2a_copy(layer, k).start()

        for copy in halos:
            copy.wait_recv()
        carry[:, :, :LANES] = jnp.zeros((2, pair, LANES), f32)
        carry[:, :, LANES + cols :] = jnp.zeros((2, pair, LANES), f32)

        @pl.loop(0, groups)
        def _(g):
            before, after = hcol[layer, 0].astype(f32), hcol[layer, 1].astype(f32)
            heads, tails = [], []
            for p in range(2):
                k = 2 * g + p
                heads.append(pltpu.roll(before, (2 * LANES - 4 - 4 * k) % LANES, 1))
                tails.append(pltpu.roll(after, (LANES - 4 * k) % LANES, 1))
            store_rows(g, heads[0], heads[1], 0)
            store_rows(g, tails[0], tails[1], LANES + cols)

        above, below = hrow[layer, 0].astype(f32), hrow[layer, 1].astype(f32)

        def patch(ref_rows, halo):
            return jnp.concatenate([halo, ref_rows.astype(f32)[pair:]], axis=0).astype(bf16)

        nst[: 2 * pair, :] = patch(nst[: 2 * pair, :], above[pair:])
        end = groups * whole
        nst[end : end + 2 * pair, :] = jnp.concatenate([carry[1], below[:pair]], axis=0).astype(bf16)
        end = groups * half
        for p in range(2):
            side = slice(p * pair, (p + 1) * pair)
            fst[p, : 2 * pair, :] = patch(fst[p, : 2 * pair, :], above[side])
            fst[p, end : end + 2 * pair, :] = jnp.concatenate(
                [carry[p], below[side]], axis=0
            ).astype(bf16)

        cut = first_part * groups // 16

        @pl.loop(0, cut)
        def _(g):
            conv_group(layer, g)

        mix_modes(layer)

        @pl.loop(cut, groups)
        def _(g):
            conv_group(layer, g)

        inverse_rows(layer)
        carry[...] = jnp.zeros_like(carry)
        pack[...] = jnp.zeros_like(pack)

        @pl.loop(0, groups)
        def _(g):
            finish_group(layer, g)

        for copy in halos:
            copy.wait_send()

        @pl.loop(1, devices)
        def _(k):
            a2a_copy(layer, k).wait_send()
            gather_copy(layer, k).wait_send()


def main_call(u, weights, near, far, order, back, fwd, ftab, itab, inv, bias, mixture, sizes):
    channels, local_rows, cols = u.shape
    layers = weights.shape[0]
    devices = sizes[0] * sizes[1]
    pair = 2 * channels
    slot = (channels + 7) // 8 * 8
    blocks = devices * min(weights.shape[-1], MODES_Y) // MODES_Y
    groups = local_rows // GROUP
    wide = cols + 2 * LANES
    vmem = pl.BlockSpec(memory_space=pltpu.VMEM)
    smem = pl.BlockSpec(memory_space=pltpu.SMEM)
    dma = pltpu.SemaphoreType.DMA
    return pl.pallas_call(
        functools.partial(main_kernel, sizes=sizes, first_part=8),
        name="operator",
        out_shape=jax.ShapeDtypeStruct(u.shape, bf16),
        in_specs=[vmem] * 11 + [smem],
        out_specs=vmem,
        scratch_shapes=[
            pltpu.VMEM((groups * 8 * pair + 2 * pair, wide), bf16),
            pltpu.VMEM((2, groups * 4 * pair + 2 * pair, wide), bf16),
            pltpu.VMEM((groups * 8 * pair, cols), f32),
            pltpu.VMEM((groups * 8 * pair, LANES), f32),
            pltpu.VMEM((groups * 8 * pair, LANES), f32),
            pltpu.VMEM((2, pair, wide), f32),
            pltpu.VMEM((2, 4 * pair, LANES), f32),
            pltpu.VMEM((layers, 2, 4 * pair, LANES), bf16),
            pltpu.VMEM((layers, 2, 2 * pair, cols), bf16),
            pltpu.VMEM((layers, 2, 4 * pair, LANES), bf16),
            pltpu.VMEM((layers, 2, 2 * pair, wide), bf16),
            pltpu.VMEM((layers, blocks * slot, LANES), f32),
            pltpu.VMEM((layers, devices - 1, slot, LANES), f32),
            pltpu.VMEM((layers, slot, LANES), f32),
            pltpu.VMEM((layers, devices * slot, LANES), f32),
            dma((layers, 8)),
            dma((layers, 8)),
            dma((layers, devices - 1)),
            dma((layers, devices - 1)),
            dma((layers, devices - 1)),
            dma((layers, devices - 1)),
        ],
        compiler_params=pltpu.CompilerParams(
            collective_id=0, has_side_effects=True, vmem_limit_bytes=62 * 1024 * 1024
        ),
    )(u, weights, near, far, order, back, fwd, ftab, itab, inv, bias, mixture)


def solution(mesh):
    sizes = (mesh.shape["gx"], mesh.shape["gy"])

    def on_device(grid_field, spectral_weight, conv_near, conv_far, mix_logits, channel_bias):
        _, channels, local_rows, local_cols = grid_field.shape
        share = spectral_weight.shape[-1]
        devices = sizes[0] * sizes[1]
        cells_x, cells_y = local_rows * sizes[0], local_cols * sizes[1]
        modes_x = share * devices // MODES_Y
        per_share = max(share // MODES_Y, 1)
        blocks = modes_x // per_share
        groups = local_rows // GROUP
        assert share * per_share in (16, 32, 128)
        assert groups * GROUP == local_rows and 8 * groups <= LANES

        lower = jnp.arange(modes_x // 2, dtype=jnp.int32)
        row_modes = jnp.concatenate([lower, lower + (cells_x - modes_x // 2)])
        row_modes = row_modes.reshape(blocks, per_share).T.reshape(modes_x)
        col_modes = jnp.arange(MODES_Y, dtype=jnp.int32)
        index = jnp.arange(local_rows, dtype=jnp.int32)
        inner = index % GROUP
        in_group = (inner % 8) // 2 * 4 + inner % 2 * 2 + inner // 8
        row_at = lax.axis_index("gx") * local_rows + index // GROUP * GROUP + in_group
        col_at = lax.axis_index("gy") * local_cols + jnp.arange(local_cols, dtype=jnp.int32)
        row_phase = (row_modes[:, None] * row_at[None, :] % cells_x).astype(f32) * (
            full_turn / cells_x
        )
        row_table = jnp.concatenate([jnp.cos(row_phase), jnp.sin(row_phase)], axis=0)
        high, low = split_bf16(row_table)
        ftab = jnp.concatenate([high, high, low], axis=1)
        itab = jnp.concatenate([high.T, high.T, low.T], axis=1)
        col_phase = (col_at[:, None] * col_modes[None, :] % cells_y).astype(f32) * (
            full_turn / cells_y
        )
        cosine, sine = jnp.cos(col_phase), -jnp.sin(col_phase)
        fwd = jnp.concatenate([cosine, sine, sine, -cosine], axis=1).astype(bf16)
        col_weight = jnp.where(col_modes == 0, 1.0, 2.0).astype(f32) / (cells_x * cells_y)
        inverse = jnp.concatenate([cosine * col_weight, sine * col_weight], axis=1).T
        high, low = split_bf16(inverse)
        inv = jnp.concatenate([high, high, low], axis=0)

        at = jnp.arange(GROUP * channels, dtype=jnp.int32)
        inner = at // channels
        natural = at % channels * GROUP + (inner % 8) // 2 * 4 + inner % 2 * 2 + inner // 8
        order = (natural[:, None] == at[None, :]).astype(bf16)
        back = (natural[None, :] == at[:, None]).astype(bf16)

        exponents = jnp.exp(mix_logits)
        mixtures = exponents / jnp.sum(exponents, axis=1, keepdims=True)
        bias = jnp.tile(channel_bias, (1, 8))[:, :, None]
        near, far = prep_call(conv_near, conv_far)
        field = main_call(
            grid_field[0], spectral_weight, near, far, order, back, fwd, ftab, itab, inv, bias,
            mixtures, sizes,
        )
        return field[None]

    in_specs = (
        P(None, None, "gx", "gy"),
        P(None, None, None, None, ("gx", "gy")),
        P(),
        P(),
        P(),
        P(),
    )
    return jax.shard_map(
        on_device,
        mesh=mesh,
        in_specs=in_specs,
        out_specs=P(None, None, "gx", "gy"),
        check_vma=False,
    )
```

profile of v0, /device:TPU:1, one launch (start us, length us, event | category | flops | bytes accessed | tf_op | source)
XLA Modules:
  0.0 183.8 jit_solution(8061879547251321358)
XLA Ops:
  0.0 0.8 exponential_reduce_fusion
  0.8 1.3 exponential_divide_fusion.mix_ref
  2.2 0.1 add_bitcast_fusion
  2.3 0.1 mul.143
  2.4 0.7 tile.8
  3.1 1.3 copy.12.near_ref
  4.4 1.4 copy.13.far_ref
  5.8 0.8 tile.10.bias_ref
  6.6 0.3 broadcast_multiply_fusion
  6.9 0.7 copy.15.fwd_ref
  7.6 0.7 pad_maximum_fusion.2.inv_ref
  8.3 0.6 fusion.10
  8.9 0.1 subtract_convert_fusion.1
  9.0 0.7 pad_maximum_fusion.1.itab_ref
  9.8 0.8 copy.16.ftab_ref
  10.6 0.9 fusion.1
  11.5 2.2 %copy.14.sw_ref = f32[2,2,20,20,64]{4,3,2,1,0:T(8,128)} copy(f32[2,2,20,20,64]{4,1,3,2,0:T(2,128)} %param.7) | data formatting | bytes 819200 | tf_op args[1]
  13.7 5.5 %prep.1 = (bf16[2,160,720]{2,1,0:T(8,128)(2,1)}, bf16[2,160,1200]{2,1,0:T(8,128)(2,1)}) custom-call(bf16[2,20,180]{2,1,0:T(8,128)(2,1)} %copy.12.near_ref, bf16[2,20,500]{2,1,0:T(8,128)(2,1)} %copy.13.far_ref), custom_call_target="tpu_custom_call" | custom-call | tf_op jit(solution)/shard_map/prep/pallas_call | solution.py:80
  19.2 159.2 %operator.1 = bf16[20,256,512]{2,1,0:T(8,128)(2,1)} custom-call(bf16[20,256,512]{2,1,0:T(8,128)(2,1)} %bitcast.15, f32[2,2,20,20,64]{4,3,2,1,0:T(8,128)} %copy.14.sw_ref, bf16[2,160,720]{2,1,0:T(8,128)(2,1)} %get-tuple-element.7.near_ref, bf16[2,160,1200]{2,1,0:T(8,128)(2,1)} %get-tuple-element.8.far_ref, bf16[320,320]{1,0:T(8,128)(2,1)} %get-tuple-element.17.order_ref, ...), custom_call_target="tpu_custom_call" | custom-call | tf_op jit(solution)/shard_map/operator/pallas_call | solution.py:441
  178.5 5.3 %copy.19 = bf16[1,20,256,512]{3,2,1,0:T(8,128)(2,1)} copy(bf16[1,20,256,512]{3,2,1,0:T(8,128)(2,1)} %bitcast.14) | data formatting | bytes 10485760
  (9 shorter events, 0.1 us)
where the time goes:
time: 185 us; the launch traced here: 184 us
  Pallas kernels  165 us (89%)
  local copies, waits for them, and re-layouts  13.3 us (7%)
  other arithmetic  5.61 us (3%)
    pallas_call x1, Pallas kernels, main_call(): pl.pallas_call(functools.partial(main_kernel, sizes=sizes, first_part=8),...  159 us
    unnamed x4, local copies, waits for them, and re-layouts  10.2 us
    pallas_call x1, Pallas kernels, prep_call(): pl.pallas_call(prep_kernel, grid=(layers,), name='prep', in_specs=[block(...  5.52 us

commit v1 on v0

v1 whole, which is shorter than its diff:
```python
import functools
import math

import jax
import jax.numpy as jnp
from jax import lax
from jax.experimental import pallas as pl
from jax.experimental.pallas import tpu as pltpu
from jax.sharding import PartitionSpec as P

full_turn = 2.0 * math.pi
MESH = pl.DeviceIdType.MESH
MODES_Y = 32
GROUP = 16
LANES = 128
HALO = 4
NEAR = (-1, 0, 1)
FAR = (-4, -2, 0, 2, 4)
f32 = jnp.float32
bf16 = jnp.bfloat16


def split_bf16(value):
    high = value.astype(bf16)
    low = (value - high.astype(f32)).astype(bf16)
    return high, low


def restore_kernel(value_ref, back_ref, columns_ref, out_ref):
    value = jnp.dot(value_ref[...], columns_ref[...], preferred_element_type=f32).astype(bf16)
    value = jnp.dot(back_ref[...], value, preferred_element_type=f32).astype(bf16)
    out_ref[...] = value.reshape(out_ref.shape)


def restore_call(value, back, columns, channels):
    whole = channels * GROUP
    groups, cols = value.shape[0] // whole, value.shape[1]
    vmem = pl.BlockSpec(memory_space=pltpu.VMEM)
    return pl.pallas_call(
        restore_kernel,
        grid=(groups,),
        name="restore",
        in_specs=[pl.BlockSpec((whole, cols), lambda i: (i, 0)), vmem, vmem],
        out_specs=pl.BlockSpec((channels, GROUP, cols), lambda i: (0, i, 0)),
        out_shape=jax.ShapeDtypeStruct((channels, groups * GROUP, cols), bf16),
    )(value, back, columns)


def main_kernel(
    u_ref, sw_ref, near_ref, far_ref, order_ref, columns_ref, stack_ref, rtab_ref, ctab_ref,
    mix_ref, bias_ref, out_ref,
    ubuf, obuf, nst, fst, conv, lhs, lines, carry, pack, packs, edges, hcol, hrow, hcorner,
    sendbuf, recv, mixed, gath, nw, fw, taps, tall, ftab, itab, fwd, inv, mixb, biasb, code, pairs,
    u_sem, out_sem, halo_send, halo_recv, a2a_send, a2a_recv, gat_send, gat_recv,
    *, sizes, cells, first_part, batch,
):
    gx, gy = sizes
    devices = gx * gy
    layers = sw_ref.shape[0]
    channels, local_rows, cols = ubuf.shape
    pair = 2 * channels
    half = 4 * pair
    whole = 2 * half
    groups = local_rows // GROUP
    planes = cols // LANES
    edge = HALO // planes
    slot = mixed.shape[1]
    blocks = sendbuf.shape[1] // slot
    sharers = devices // blocks
    per_device = 2 * MODES_Y
    modes_x = rtab_ref.shape[0] // 2
    share_rows = modes_x // blocks
    share = sw_ref.shape[-1]
    trim = (pair + 15) // 16 * 16
    my_x, my_y = lax.axis_index("gx"), lax.axis_index("gy")
    me = my_x * gy + my_y

    def place(index):
        return (index // gy, index % gy)

    barrier = pltpu.get_barrier_semaphore()

    @pl.loop(1, devices)
    def _(k):
        pl.semaphore_signal(
            barrier, inc=1, device_id=place((me + k) % devices), device_id_type=MESH
        )

    def u_copy(g):
        rows = pl.ds(pl.multiple_of(g * GROUP, GROUP), GROUP)
        return pltpu.make_async_copy(u_ref.at[:, rows, :], ubuf.at[:, rows, :], u_sem.at[g])

    @pl.loop(0, groups)
    def _(g):
        u_copy(g).start()

    def iota(shape, dim):
        return lax.broadcasted_iota(jnp.int32, shape, dim)

    high, low = split_bf16(rtab_ref[...])
    ftab[...] = jnp.concatenate([high, high, low], axis=1)
    high, low = split_bf16(rtab_ref[...].T)
    itab[...] = jnp.concatenate([high, high, low], axis=1)
    fwd[...] = ctab_ref[...].astype(bf16)
    turned_cols = ctab_ref[...].T[:per_device]
    weight = jnp.where(iota((per_device, cols), 0) % MODES_Y == 0, 1.0, 2.0) / cells
    high, low = split_bf16(turned_cols * weight)
    inv[...] = jnp.concatenate([high, high, low], axis=0)

    exponents = jnp.exp(mix_ref[...])
    mixtures = exponents / jnp.sum(exponents, axis=1, keepdims=True)
    for layer in range(layers):
        for i in range(3):
            at = 3 * layer + i
            mixb[at : at + 1, :] = jnp.broadcast_to(
                mixtures[layer : layer + 1, i : i + 1], (1, cols)
            )
        same = iota((half, channels), 0) % channels == iota((half, channels), 1)
        column = jnp.sum(
            jnp.where(same, bias_ref[layer : layer + 1, :], 0.0), axis=1, keepdims=True
        )
        biasb[layer] = jnp.broadcast_to(column, (half, LANES))

    at, lane_at = iota(code.shape, 0), iota(code.shape, 1)
    plane, lane = lane_at // LANES, lane_at % LANES
    before = planes * (lane - (LANES - edge)) + plane
    after = planes * lane + plane
    code[...] = jnp.where(
        (at < LANES) & (lane >= LANES - edge),
        at - before,
        jnp.where((at >= LANES) & (lane < edge), at - LANES - after, -1),
    )

    def edge_pick(k):
        return jnp.where(code[...] == HALO * k, 1.0, 0.0).astype(bf16)

    depth = 6 * pair
    wide = (depth + LANES - 1) // LANES * LANES

    def tap_rows(taps_ref):
        count = taps_ref.shape[2]
        for o in range(channels):
            taps[layers * o : layers * (o + 1), :count] = taps_ref[o].astype(f32)
        return taps[:, :count].astype(bf16)

    rows_of = layers * channels

    def spread(out_ref, index):
        stacked = tall[...].astype(bf16)
        full = jnp.dot(stack_ref[...], stacked, preferred_element_type=f32).astype(bf16)
        return [full[layer * half : (layer + 1) * half, :depth] for layer in range(layers)]

    def emit(out_ref, pieces):
        for layer in range(layers):
            out_ref[layer] = jnp.concatenate([piece[layer] for piece in pieces], axis=1)

    source = tap_rows(far_ref)
    count = far_ref.shape[2]
    target = iota((count, wide), 1)
    base = jnp.where(
        target < 5 * channels,
        target // channels * (5 * channels) + target % channels,
        -count,
    )
    base = iota((count, wide), 0) - base
    pieces = []
    for column in range(5):
        pick = jnp.where(base == column * channels, 1.0, 0.0).astype(bf16)
        block = jnp.dot(source, pick, preferred_element_type=f32)
        for row in range(8):
            tall[rows_of * row : rows_of * (row + 1), :] = (
                pltpu.roll(block, channels * row, 1) if row else block
            )
        pieces.append(spread(fw, column))
    emit(fw, pieces)

    source = tap_rows(near_ref)
    count = near_ref.shape[2]
    target = iota((count, wide), 1)
    spot, channel = target // channels, target % channels
    where_row = {-1: 1, 0: 2, 1: 4, 2: 3, 3: 5, 4: 6}
    bases = []
    for row in range(4):
        tap = jnp.full(target.shape, -count, jnp.int32)
        for step in range(3):
            tap = jnp.where(
                spot == where_row[row + step - 1], step * 3 * channels + channel, tap
            )
        bases.append(iota((count, wide), 0) - tap)
    pieces = []
    for column in range(3):
        for row in range(4):
            pick = jnp.where(bases[row] == column * channels, 1.0, 0.0).astype(bf16)
            block = jnp.dot(source, pick, preferred_element_type=f32)
            for quad in range(2):
                full_row = 4 * quad + row
                index = full_row % 2 * 4 + full_row // 2
                tall[rows_of * index : rows_of * (index + 1), :] = (
                    pltpu.roll(block, 4 * channels, 1) if quad else block
                )
        pieces.append(spread(nw, column))
    emit(nw, pieces)

    def near_edges(value):
        low_lanes = iota((value.shape[0], LANES), 1) < LANES // 2
        return jnp.where(low_lanes, value[:, :LANES], value[:, cols - LANES :])

    def store_rows(g, even, odd, side):
        at = slice(side * cols, (side + 1) * cols)
        old_even, old_odd = carry[0, :, at], carry[1, :, at]
        q = [(even[i * pair : (i + 1) * pair], odd[i * pair : (i + 1) * pair]) for i in range(4)]
        near_rows = [old_odd]
        for i in range(4):
            near_rows.append(q[i][0])
            if i < 3:
                near_rows.append(q[i][1])
        near_rows = jnp.concatenate(near_rows, axis=0)
        near_at = pl.ds(pl.multiple_of(g * whole, whole), whole)
        if side:
            nst[near_at, cols:] = near_edges(near_rows).astype(bf16)
        else:
            nst[near_at, :cols] = near_rows.astype(bf16)
        row = pl.ds(pl.multiple_of(g * half, half), half)
        fst[0, row, at] = jnp.concatenate([old_even, even[: 3 * pair]], axis=0).astype(bf16)
        fst[1, row, at] = jnp.concatenate([old_odd, odd[: 3 * pair]], axis=0).astype(bf16)
        carry[0, :, at] = q[3][0]
        carry[1, :, at] = q[3][1]

    def ingest(g, value, layer):
        full = value.astype(f32)
        even, odd = full[:half], full[half:]
        store_rows(g, even, odd, 0)
        lines[pl.ds(pl.multiple_of(g * whole, whole), whole), :] = jnp.dot(
            value, fwd[...], preferred_element_type=f32
        )
        total = pack[...]
        for p in range(2):
            total = total + lax.dot_general(
                value[p * half : (p + 1) * half],
                edge_pick(2 * g + p),
                (((1,), (1,)), ((), ())),
                preferred_element_type=f32,
            )
        pack[...] = total

        @pl.when(g == 0)
        def _():
            edges[layer, 0] = jnp.concatenate([even[:pair], odd[:pair]], axis=0).astype(bf16)

        @pl.when(g == groups - 1)
        def _():
            edges[layer, 1] = jnp.concatenate(
                [even[3 * pair :], odd[3 * pair :]], axis=0
            ).astype(bf16)

    carry[...] = jnp.zeros_like(carry)
    pack[...] = jnp.zeros_like(pack)

    @pl.loop(0, groups)
    def _(g):
        u_copy(g).wait()
        slab = ubuf[:, pl.ds(pl.multiple_of(g * GROUP, GROUP), GROUP), :].reshape(whole, cols)
        value = jnp.dot(order_ref[...], slab, preferred_element_type=f32).astype(bf16)
        value = jnp.dot(value, columns_ref[...], preferred_element_type=f32).astype(bf16)
        ingest(g, value, 0)

    pl.semaphore_wait(barrier, devices - 1)

    up, down = (my_x + gx - 1) % gx, (my_x + 1) % gx
    left, right = (my_y + gy - 1) % gy, (my_y + 1) % gy

    def halo_copies(layer):
        def copy(i, src, dst, target):
            return pltpu.make_async_remote_copy(
                src_ref=src, dst_ref=dst, send_sem=halo_send.at[layer, i],
                recv_sem=halo_recv.at[layer, i], device_id=target, device_id_type=MESH,
            )

        mine, beside = packs.at[layer], hcol.at[layer]
        above, below = hcorner.at[layer, 0], hcorner.at[layer, 1]
        lasts, firsts = slice(0, LANES), slice(LANES, 2 * LANES)
        head, tail = slice(0, trim), slice(half - trim, half)
        return [
            copy(0, mine.at[:, firsts], beside.at[:, firsts], (my_x, left)),
            copy(1, mine.at[:, lasts], beside.at[:, lasts], (my_x, right)),
            copy(2, edges.at[layer, 0], hrow.at[layer, 1], (up, my_y)),
            copy(3, edges.at[layer, 1], hrow.at[layer, 0], (down, my_y)),
            copy(4, mine.at[head, firsts], below.at[:, firsts], (up, left)),
            copy(5, mine.at[tail, firsts], above.at[:, firsts], (down, left)),
            copy(6, mine.at[head, lasts], below.at[:, lasts], (up, right)),
            copy(7, mine.at[tail, lasts], above.at[:, lasts], (down, right)),
        ]

    def a2a_copy(layer, k):
        target = (me + k) % devices
        return pltpu.make_async_remote_copy(
            src_ref=sendbuf.at[layer, pl.ds(target // sharers * slot, slot)],
            dst_ref=recv.at[layer, k - 1],
            send_sem=a2a_send.at[layer, k - 1],
            recv_sem=a2a_recv.at[layer, k - 1],
            device_id=place(target),
            device_id_type=MESH,
        )

    def gather_copy(layer, k):
        return pltpu.make_async_remote_copy(
            src_ref=mixed.at[layer],
            dst_ref=gath.at[layer, pl.ds(me * slot, slot)],
            send_sem=gat_send.at[layer, k - 1],
            recv_sem=gat_recv.at[layer, k - 1],
            device_id=place((me + k) % devices),
            device_id_type=MESH,
        )

    def turned(value):
        return jnp.where(
            (iota(value.shape, 1) // MODES_Y) % 2 == 1,
            pltpu.roll(value, MODES_Y, 1),
            -pltpu.roll(value, LANES - MODES_Y, 1),
        )

    def triple(value):
        high, low = split_bf16(value)
        return jnp.concatenate([high, low, high], axis=0)

    def row_transform(layer):
        @pl.loop(0, channels // batch)
        def _(b):
            parts = [
                triple(lines[pl.ds(b * batch + i, local_rows, stride=channels), :])
                for i in range(batch)
            ]
            result = jnp.dot(
                ftab[...], jnp.concatenate(parts, axis=1), preferred_element_type=f32
            )
            for i in range(batch):
                both = result[:, i * LANES : (i + 1) * LANES]
                total = both[:modes_x] + pltpu.roll(both[modes_x:], per_device, 1)
                block = total
                if share_rows == 2:
                    block = jnp.where(
                        iota((blocks, LANES), 1) < per_device,
                        total[:blocks],
                        pltpu.roll(total[blocks:], per_device, 1),
                    )
                sendbuf[layer, pl.ds(b * batch + i, blocks, stride=slot), :] = block

    def mix_modes(layer):
        own = sendbuf[layer, pl.ds(pl.multiple_of(me // sharers * slot, 8), slot), :]

        @pl.loop(1, devices)
        def _(k):
            a2a_copy(layer, k).wait_recv()

        own = own + jnp.sum(recv[layer], axis=0)
        crossed = turned(own)
        is_real = iota((2 * channels, LANES), 0) % 2 == 0

        def spread_lanes(part):
            if share_rows == 1:
                tiled = jnp.concatenate([part] * (LANES // share), axis=1)
                at = iota(tiled.shape, 1) // share
                return jnp.where(at % sharers == me % sharers, tiled, 0.0)
            pieces = []
            for j in range(share_rows):
                piece = part[:, j * MODES_Y : (j + 1) * MODES_Y]
                pieces += [piece, piece]
            return jnp.concatenate(pieces, axis=1)

        total = jnp.zeros((2 * channels, LANES), f32)
        for c in range(channels):
            weights = spread_lanes(sw_ref[layer, c].reshape(2 * channels, share))
            total = total + weights * jnp.where(is_real, own[c : c + 1], crossed[c : c + 1])
        pairs[...] = total
        total = pairs[pl.ds(0, channels, stride=2), :] + pairs[pl.ds(1, channels, stride=2), :]
        total = total * mixb[3 * layer : 3 * layer + 1, :LANES]
        mixed[layer, :channels, :] = total
        gath[layer, pl.ds(pl.multiple_of(me * slot, 8), channels), :] = total

        @pl.loop(1, devices)
        def _(k):
            gather_copy(layer, k).start()

    def inverse_rows(layer):
        @pl.loop(1, devices)
        def _(k):
            gather_copy(layer, k).wait_recv()

        @pl.loop(0, channels // batch)
        def _(b):
            parts = []
            for i in range(batch):
                o = b * batch + i
                block = gath[layer, pl.ds(o, blocks, stride=slot * sharers), :]
                for j in range(1, sharers):
                    block = block + gath[layer, pl.ds(j * slot + o, blocks, stride=slot * sharers), :]
                cross = turned(block)
                stack = [block, cross]
                if share_rows == 2:
                    stack = [block, pltpu.roll(block, per_device, 1)]
                    stack += [cross, pltpu.roll(cross, per_device, 1)]
                parts.append(triple(jnp.concatenate(stack, axis=0)))
            result = jnp.dot(
                itab[...], jnp.concatenate(parts, axis=1), preferred_element_type=f32
            )
            for i in range(batch):
                lhs[pl.ds(b * batch + i, local_rows, stride=channels), :] = result[
                    :, i * LANES : (i + 1) * LANES
                ]

    def conv_group(layer, g):
        def window(rows, shifts, beside):
            own = [rows[:, s * LANES : (s + 1) * LANES] for s in range(planes)]
            at = iota((depth, LANES), 1)
            known = {}

            def piece(s, d):
                q = s + d
                plane, move = q % planes, q // planes
                if (plane, move) not in known:
                    value = own[plane]
                    if move > 0:
                        value = jnp.where(at < move, beside(plane), value)
                    if move < 0:
                        value = jnp.where(at >= LANES + move, beside(plane), value)
                    if move:
                        value = pltpu.roll(value, (-move) % LANES, 1)
                    known[plane, move] = value
                return known[plane, move]

            return jnp.concatenate(
                [
                    jnp.concatenate([piece(s, d) for s in range(planes)], axis=1)
                    for d in shifts
                ],
                axis=0,
            )

        near = []
        for h in range(2):
            rows = nst[pl.ds(pl.multiple_of(g * whole, whole) + h * half, depth), :]
            columns = window(rows, NEAR, lambda plane: rows[:, cols:])
            near.append(jnp.dot(nw[layer], columns, preferred_element_type=f32))
        parts = []
        bias = jnp.concatenate([biasb[layer]] * planes, axis=1)
        for p in range(2):
            rows = fst[p, pl.ds(pl.multiple_of(g * half, half), depth), :]
            columns = window(
                rows, FAR, lambda s: rows[:, cols + s * LANES : cols + (s + 1) * LANES]
            )
            far = jnp.dot(fw[layer], columns, preferred_element_type=f32)
            side = slice(p * 2 * pair, (p + 1) * 2 * pair)
            close = jnp.concatenate([near[0][side], near[1][side]], axis=0)
            total = (
                mixb[3 * layer + 1 : 3 * layer + 2, :] * close
                + mixb[3 * layer + 2 : 3 * layer + 3, :] * far
                + bias
            )
            parts.append(total)
        conv[pl.ds(pl.multiple_of(g * whole, whole), whole), :] = jnp.concatenate(parts, axis=0)

    def out_copy(g):
        rows = pl.ds(pl.multiple_of(g * whole, whole), whole)
        return pltpu.make_async_copy(obuf.at[rows], out_ref.at[rows], out_sem.at[g])

    def finish_group(layer, g):
        at = pl.ds(pl.multiple_of(g * whole, whole), whole)
        high, low = split_bf16(lhs[at, :per_device])
        spectral = jnp.dot(
            jnp.concatenate([high, low, high], axis=1), inv[...], preferred_element_type=f32
        )
        value = conv[at, :] + spectral
        value = (value * 0.5 * (1.0 + lax.erf(value * (0.5**0.5)))).astype(bf16)
        if layer + 1 < layers:
            ingest(g, value, layer + 1)
        else:
            obuf[at, :] = value
            out_copy(g).start()

    for layer in range(layers):
        packs[layer] = pack[...].astype(bf16)
        halos = halo_copies(layer)
        for copy in halos:
            copy.start()
        row_transform(layer)

        @pl.loop(1, devices)
        def _(k):
            a2a_copy(layer, k).start()

        for copy in halos:
            copy.wait_recv()
        carry[:, :, cols:] = jnp.zeros((2, pair, cols), f32)

        @pl.loop(0, groups)
        def _(g):
            beside = hcol[layer]
            parts = [
                jnp.dot(beside, edge_pick(2 * g + p), preferred_element_type=f32)
                for p in range(2)
            ]
            store_rows(g, parts[0], parts[1], 1)

        def halo_rows(side):
            k = 0 if side else 2 * (groups - 1)
            main = hrow[layer, side].astype(f32)
            out = []
            for p in range(2):
                corner = jnp.dot(
                    hcorner[layer, side], edge_pick(k + p), preferred_element_type=f32
                )
                corner = corner[:pair] if side else corner[trim - pair :]
                out.append((main[p * pair : (p + 1) * pair], corner))
            return out

        above, below = halo_rows(0), halo_rows(1)
        first = slice(0, 2 * pair)

        def patch(rows, halo):
            return jnp.concatenate([halo, rows.astype(f32)[pair:]], axis=0).astype(bf16)

        nst[first, :cols] = patch(nst[first, :cols], above[1][0])
        nst[first, cols:] = patch(nst[first, cols:], near_edges(above[1][1]))
        end = groups * whole
        last = slice(end, end + 2 * pair)
        nst[last, :cols] = jnp.concatenate([carry[1, :, :cols], below[0][0]], axis=0).astype(bf16)
        nst[last, cols:] = near_edges(
            jnp.concatenate([carry[1, :, cols:], below[0][1]], axis=0)
        ).astype(bf16)
        end = groups * half
        last = slice(end, end + 2 * pair)
        for p in range(2):
            for side in range(2):
                at = slice(side * cols, (side + 1) * cols)
                fst[p, first, at] = patch(fst[p, first, at], above[p][side])
                fst[p, last, at] = jnp.concatenate(
                    [carry[p, :, at], below[p][side]], axis=0
                ).astype(bf16)

        cut = first_part * groups // 16

        @pl.loop(0, cut)
        def _(g):
            conv_group(layer, g)

        mix_modes(layer)

        @pl.loop(cut, groups)
        def _(g):
            conv_group(layer, g)

        inverse_rows(layer)
        carry[...] = jnp.zeros_like(carry)
        pack[...] = jnp.zeros_like(pack)

        @pl.loop(0, groups)
        def _(g):
            finish_group(layer, g)

        for copy in halos:
            copy.wait_send()

        @pl.loop(1, devices)
        def _(k):
            a2a_copy(layer, k).wait_send()
            gather_copy(layer, k).wait_send()

    @pl.loop(0, groups)
    def _(g):
        out_copy(g).wait()


def main_call(u, weights, near, far, order, columns, stack, rtab, ctab, mix, bias, sizes, cells):
    channels, local_rows, cols = u.shape
    layers = weights.shape[0]
    devices = sizes[0] * sizes[1]
    pair = 2 * channels
    half = 4 * pair
    slot = (channels + 7) // 8 * 8
    blocks = devices * min(weights.shape[-1], MODES_Y) // MODES_Y
    groups = local_rows // GROUP
    modes_x = rtab.shape[0] // 2
    depth = 6 * pair
    wide = (depth + LANES - 1) // LANES * LANES
    trim = (pair + 15) // 16 * 16
    vmem = pl.BlockSpec(memory_space=pltpu.VMEM)
    anywhere = pl.BlockSpec(memory_space=pl.ANY)
    dma = pltpu.SemaphoreType.DMA
    scratch = pltpu.VMEM
    return pl.pallas_call(
        functools.partial(
            main_kernel, sizes=sizes, cells=cells, first_part=8,
            batch=4 if channels % 4 == 0 else 1,
        ),
        name="operator",
        out_shape=jax.ShapeDtypeStruct((groups * 2 * half, cols), bf16),
        in_specs=[anywhere] + [vmem] * 10,
        out_specs=anywhere,
        scratch_shapes=[
            scratch((channels, local_rows, cols), bf16),
            scratch((groups * 2 * half, cols), bf16),
            scratch((groups * 2 * half + 2 * pair, cols + LANES), bf16),
            scratch((2, groups * half + 2 * pair, 2 * cols), bf16),
            scratch((groups * 2 * half, cols), f32),
            scratch((groups * 2 * half, LANES), f32),
            scratch((groups * 2 * half, LANES), f32),
            scratch((2, pair, 2 * cols), f32),
            scratch((half, 2 * LANES), f32),
            scratch((layers, half, 2 * LANES), bf16),
            scratch((layers, 2, 2 * pair, cols), bf16),
            scratch((layers, half, 2 * LANES), bf16),
            scratch((layers, 2, 2 * pair, cols), bf16),
            scratch((layers, 2, trim, 2 * LANES), bf16),
            scratch((layers, blocks * slot, LANES), f32),
            scratch((layers, devices - 1, slot, LANES), f32),
            scratch((layers, slot, LANES), f32),
            scratch((layers, devices * slot, LANES), f32),
            scratch((layers, half, 3 * depth), bf16),
            scratch((layers, half, 5 * depth), bf16),
            scratch((layers * channels, 4 * LANES), f32),
            scratch((8 * layers * channels, wide), f32),
            scratch((2 * modes_x, 3 * local_rows), bf16),
            scratch((local_rows, 6 * modes_x), bf16),
            scratch((cols, LANES), bf16),
            scratch((6 * MODES_Y, cols), bf16),
            scratch((8, cols), f32),
            scratch((layers, half, LANES), f32),
            scratch((2 * LANES, cols), jnp.int32),
            scratch((2 * channels, LANES), f32),
            dma((groups,)),
            dma((groups,)),
            dma((layers, 8)),
            dma((layers, 8)),
            dma((layers, devices - 1)),
            dma((layers, devices - 1)),
            dma((layers, devices - 1)),
            dma((layers, devices - 1)),
        ],
        compiler_params=pltpu.CompilerParams(
            collective_id=0, has_side_effects=True, vmem_limit_bytes=62 * 1024 * 1024
        ),
    )(u, weights, near, far, order, columns, stack, rtab, ctab, mix, bias)


def solution(mesh):
    sizes = (mesh.shape["gx"], mesh.shape["gy"])

    def on_device(grid_field, spectral_weight, conv_near, conv_far, mix_logits, channel_bias):
        _, channels, local_rows, local_cols = grid_field.shape
        layers = spectral_weight.shape[0]
        share = spectral_weight.shape[-1]
        devices = sizes[0] * sizes[1]
        cells_x, cells_y = local_rows * sizes[0], local_cols * sizes[1]
        modes_x = share * devices // MODES_Y
        per_share = max(share // MODES_Y, 1)
        blocks = modes_x // per_share
        groups = local_rows // GROUP
        planes = local_cols // LANES
        assert share * per_share in (16, 32, 128)
        assert groups * GROUP == local_rows and 8 * groups <= LANES
        assert planes * LANES == local_cols and planes in (1, 2, 4)

        def group_order(inner):
            return inner % 8 // 2 * 4 + inner % 2 * 2 + inner // 8

        mode = jnp.arange(2 * modes_x, dtype=jnp.int32)
        slot = mode % modes_x % blocks * per_share + mode % modes_x // blocks
        row_mode = jnp.where(slot < modes_x // 2, slot, slot + (cells_x - modes_x))
        index = jnp.arange(local_rows, dtype=jnp.int32)
        row_at = index // GROUP * GROUP + group_order(index % GROUP)
        row_at = row_at + lax.axis_index("gx") * local_rows
        phase = (row_mode[:, None] * row_at[None, :] % cells_x).astype(f32) * (full_turn / cells_x)
        rtab = jnp.where(mode[:, None] < modes_x, jnp.cos(phase), jnp.sin(phase))

        index = jnp.arange(local_cols, dtype=jnp.int32)
        spot = index % LANES * planes + index // LANES
        col_at = lax.axis_index("gy") * local_cols + spot
        lane = jnp.arange(LANES, dtype=jnp.int32)[None, :]
        phase = (col_at[:, None] * (lane % MODES_Y) % cells_y).astype(f32) * (full_turn / cells_y)
        cosine, sine = jnp.cos(phase), jnp.sin(phase)
        kind = lane // MODES_Y
        ctab = jnp.where(kind == 0, cosine, jnp.where(kind == 3, -cosine, -sine))

        at = jnp.arange(GROUP * channels, dtype=jnp.int32)
        natural = at % channels * GROUP + group_order(at // channels)
        order = (natural[:, None] == at[None, :]).astype(bf16)
        back = (natural[None, :] == at[:, None]).astype(bf16)
        columns = (index[:, None] == spot[None, :]).astype(bf16)
        columns_back = (index[None, :] == spot[:, None]).astype(bf16)
        count = 8 * channels
        at = jnp.arange(layers * count, dtype=jnp.int32)
        wanted = at % count // channels * (layers * channels)
        wanted = wanted + at % channels * layers + at // count
        stack = (wanted[:, None] == at[None, :]).astype(bf16)

        field = main_call(
            grid_field[0],
            spectral_weight.transpose(0, 2, 3, 1, 4),
            conv_near.transpose(1, 0, 2),
            conv_far.transpose(1, 0, 2),
            order, columns, stack, rtab, ctab, mix_logits, channel_bias,
            sizes, cells_x * cells_y,
        )
        return restore_call(field, back, columns_back, channels)[None]

    in_specs = (
        P(None, None, "gx", "gy"),
        P(None, None, None, None, ("gx", "gy")),
        P(),
        P(),
        P(),
        P(),
    )
    return jax.shard_map(
        on_device,
        mesh=mesh,
        in_specs=in_specs,
        out_specs=P(None, None, "gx", "gy"),
        check_vma=False,
    )
```

time: 185 us -> 126 us (0.68)
  Pallas kernels: 165 us -> 121 us
  local copies, waits for them, and re-layouts: 13.3 us -> 0 us
    pallas_call x2, Pallas kernels: 165 us -> 121 us  [the longest x1 105 us: main_call(): pl.pallas_call(functools.partial(main_kernel, sizes=sizes, cells=cells, f...]
    unnamed x4 -> x0, local copies, waits for them, and re-layouts: 10.2 us -> none
    select_n x0 -> x4, other arithmetic: none -> 3.17 us  [the longest x1 1.91 us: on_device(): ctab = jnp.where(kind == 0, cosine, jnp.where(kind == 3, -cosine, -sine))]
where the time goes in v1:
time: 126 us
  Pallas kernels  121 us (96%)
  other arithmetic  5.41 us (4%)
    pallas_call x1, Pallas kernels, main_call(): pl.pallas_call(functools.partial(main_kernel, sizes=sizes, cells=cells, f...  105 us
    pallas_call x1, Pallas kernels, restore_call(): pl.pallas_call(restore_kernel, grid=(groups,), name='restore', in_specs=[...  15.5 us

profile of v1, /device:TPU:1, one launch (start us, length us, event | category | flops | bytes accessed | tf_op | source)
XLA Modules:
  0.0 126.0 jit_solution(16225219157182973606)
XLA Ops:
  0.1 1.2 sine_select_fusion.rtab_ref
  1.4 1.9 %select_select_fusion.ctab_ref = f32[512,128]{1,0:T(8,128)} fusion(s32[128]{0:T(128)S(1)} %and_select_fusion, s32[512]{0:T(512)S(1)} %broadcast_add_fusion, pred[128]{0:T(512)(128)(4,1)S(1)} %get-tuple-element.9, pred[128]{0:T(512)(128)(4,1)S(1)} %get-tuple-element.10), kind=kLoop, calls=%fused_computation.18 | loop fusion | flops 1179648 | bytes 264960 | tf_op jit(solution)/shard_map/jit(_where)/select_n | solution.py:682
  3.3 1.0 fusion.4
  4.3 1.1 fusion.1
  5.5 105.0 %operator.1.value_ref = bf16[5120,512]{1,0:T(8,128)(2,1)} custom-call(bf16[20,256,512]{2,1,0:T(8,128)(2,1)} %bitcast.5, f32[2,20,20,2,64]{4,3,2,1,0:T(2,128)} %bitcast.6, bf16[20,2,180]{2,1,0:T(2,128)(2,1)} %bitcast.8, bf16[20,2,500]{2,1,0:T(2,128)(2,1)} %bitcast.7, bf16[320,320]{1,0:T(8,128)(2,1)} %get-tuple-element.8.order_ref, ...), custom_call_target="tpu_custom_call" | custom-call | tf_op jit(solution)/shard_map/operator/pallas_call | solution.py:590
  110.4 15.5 %restore.1 = bf16[20,256,512]{2,1,0:T(8,128)(2,1)} custom-call(bf16[5120,512]{1,0:T(8,128)(2,1)} %operator.1.value_ref, bf16[320,320]{1,0:T(8,128)(2,1)} %get-tuple-element.7.back_ref, bf16[512,512]{1,0:T(8,128)(2,1)} %get-tuple-element.5.columns_ref), custom_call_target="tpu_custom_call" | custom-call | tf_op jit(solution)/shard_map/restore/pallas_call | solution.py:39
  (9 shorter events, 0.1 us)

commit v2 on v1

--- a/solution.py
+++ b/solution.py
@@ -14,6 +14,7 @@
 GROUP = 16
 LANES = 128
 HALO = 4
+CHUNK = 4
 NEAR = (-1, 0, 1)
 FAR = (-4, -2, 0, 2, 4)
 f32 = jnp.float32
@@ -26,31 +27,65 @@
     return high, low
 
 
-def restore_kernel(value_ref, back_ref, columns_ref, out_ref):
-    value = jnp.dot(value_ref[...], columns_ref[...], preferred_element_type=f32).astype(bf16)
-    value = jnp.dot(back_ref[...], value, preferred_element_type=f32).astype(bf16)
-    out_ref[...] = value.reshape(out_ref.shape)
-
-
-def restore_call(value, back, columns, channels):
+def group_order(place):
+    return place % 8 // 2 * 4 + place % 2 * 2 + place // 8
+
+
+def iota(shape, dim):
+    return lax.broadcasted_iota(jnp.int32, shape, dim)
+
+
+def natural_order(at, channels):
+    return at % channels * GROUP + group_order(at // channels)
+
+
+def natural_column(at, cols):
+    return at % LANES * (cols // LANES) + at // LANES
+
+
+def matches(left, right):
+    return jnp.where(left == right, 1.0, 0.0).astype(bf16)
+
+
+def restore_kernel(value_ref, out_ref, back, columns, *, chunk):
+    channels, _, cols = out_ref.shape
+    whole = channels * GROUP
+
+    @pl.when(pl.program_id(0) == 0)
+    def _():
+        at = natural_order(iota((8, whole), 1), channels)[:1]
+        back[...] = matches(iota((whole, whole), 0), at)
+        at = natural_column(iota((cols, LANES), 0), cols)[:, :1]
+        columns[...] = matches(at, iota((cols, cols), 1))
+
+    for i in range(chunk):
+        value = value_ref[i * whole : (i + 1) * whole, :]
+        value = jnp.dot(value, columns[...], preferred_element_type=f32).astype(bf16)
+        value = jnp.dot(back[...], value, preferred_element_type=f32).astype(bf16)
+        out_ref[:, i * GROUP : (i + 1) * GROUP, :] = value.reshape(channels, GROUP, cols)
+
+
+def restore_call(value, channels):
     whole = channels * GROUP
     groups, cols = value.shape[0] // whole, value.shape[1]
-    vmem = pl.BlockSpec(memory_space=pltpu.VMEM)
+    chunk = CHUNK if groups % CHUNK == 0 else 1
     return pl.pallas_call(
-        restore_kernel,
-        grid=(groups,),
+        functools.partial(restore_kernel, chunk=chunk),
+        grid=(groups // chunk,),
         name="restore",
-        in_specs=[pl.BlockSpec((whole, cols), lambda i: (i, 0)), vmem, vmem],
-        out_specs=pl.BlockSpec((channels, GROUP, cols), lambda i: (0, i, 0)),
+        in_specs=[pl.BlockSpec((chunk * whole, cols), lambda i: (i, 0))],
+        out_specs=pl.BlockSpec((channels, chunk * GROUP, cols), lambda i: (0, i, 0)),
         out_shape=jax.ShapeDtypeStruct((channels, groups * GROUP, cols), bf16),
-    )(value, back, columns)
+        scratch_shapes=[pltpu.VMEM((whole, whole), bf16), pltpu.VMEM((cols, cols), bf16)],
+    )(value)
 
 
 def main_kernel(
-    u_ref, sw_ref, near_ref, far_ref, order_ref, columns_ref, stack_ref, rtab_ref, ctab_ref,
+    u_ref, sw_ref, near_ref, far_ref, rtab_ref, ctab_ref,
     mix_ref, bias_ref, out_ref,
     ubuf, obuf, nst, fst, conv, lhs, lines, carry, pack, packs, edges, hcol, hrow, hcorner,
     sendbuf, recv, mixed, gath, nw, fw, taps, tall, ftab, itab, fwd, inv, mixb, biasb, code, pairs,
+    order, columns, stack,
     u_sem, out_sem, halo_send, halo_recv, a2a_send, a2a_recv, gat_send, gat_recv,
     *, sizes, cells, first_part, batch,
 ):
@@ -94,8 +129,13 @@
     def _(g):
         u_copy(g).start()
 
-    def iota(shape, dim):
-        return lax.broadcasted_iota(jnp.int32, shape, dim)
+    at = natural_order(iota((whole, LANES), 0), channels)[:, :1]
+    order[...] = matches(at, iota((whole, whole), 1))
+    at = natural_column(iota((8, cols), 1), cols)[:1]
+    columns[...] = matches(iota((cols, cols), 0), at)
+    at = iota((layers * half, LANES), 0)
+    wanted = at % half // channels * (layers * channels) + at % channels * layers + at // half
+    stack[...] = matches(wanted[:, :1], iota(stack.shape, 1))
 
     high, low = split_bf16(rtab_ref[...])
     ftab[...] = jnp.concatenate([high, high, low], axis=1)
@@ -147,7 +187,7 @@
 
     def spread(out_ref, index):
         stacked = tall[...].astype(bf16)
-        full = jnp.dot(stack_ref[...], stacked, preferred_element_type=f32).astype(bf16)
+        full = jnp.dot(stack[...], stacked, preferred_element_type=f32).astype(bf16)
         return [full[layer * half : (layer + 1) * half, :depth] for layer in range(layers)]
 
     def emit(out_ref, pieces):
@@ -256,12 +296,12 @@
     carry[...] = jnp.zeros_like(carry)
     pack[...] = jnp.zeros_like(pack)
 
-    @pl.loop(0, groups)
+    @pl.loop(0, groups, unroll=2)
     def _(g):
         u_copy(g).wait()
         slab = ubuf[:, pl.ds(pl.multiple_of(g * GROUP, GROUP), GROUP), :].reshape(whole, cols)
-        value = jnp.dot(order_ref[...], slab, preferred_element_type=f32).astype(bf16)
-        value = jnp.dot(value, columns_ref[...], preferred_element_type=f32).astype(bf16)
+        value = jnp.dot(order[...], slab, preferred_element_type=f32).astype(bf16)
+        value = jnp.dot(value, columns[...], preferred_element_type=f32).astype(bf16)
         ingest(g, value, 0)
 
     pl.semaphore_wait(barrier, devices - 1)
@@ -488,11 +528,11 @@
         def _(k):
             a2a_copy(layer, k).start()
 
-        for copy in halos:
+        for copy in halos[:2]:
             copy.wait_recv()
         carry[:, :, cols:] = jnp.zeros((2, pair, cols), f32)
 
-        @pl.loop(0, groups)
+        @pl.loop(0, groups, unroll=2)
         def _(g):
             beside = hcol[layer]
             parts = [
@@ -500,6 +540,21 @@
                 for p in range(2)
             ]
             store_rows(g, parts[0], parts[1], 1)
+
+        cut = 1 + first_part * (groups - 2) // 14
+
+        @pl.loop(1, cut)
+        def _(g):
+            conv_group(layer, g)
+
+        mix_modes(layer)
+
+        @pl.loop(cut, groups - 1)
+        def _(g):
+            conv_group(layer, g)
+
+        for copy in halos[2:]:
+            copy.wait_recv()
 
         def halo_rows(side):
             k = 0 if side else 2 * (groups - 1)
@@ -537,23 +592,15 @@
                     [carry[p, :, at], below[p][side]], axis=0
                 ).astype(bf16)
 
-        cut = first_part * groups // 16
-
-        @pl.loop(0, cut)
-        def _(g):
-            conv_group(layer, g)
-
-        mix_modes(layer)
-
-        @pl.loop(cut, groups)
-        def _(g):
-            conv_group(layer, g)
+        @pl.loop(0, 2)
+        def _(i):
+            conv_group(layer, i * (groups - 1))
 
         inverse_rows(layer)
         carry[...] = jnp.zeros_like(carry)
         pack[...] = jnp.zeros_like(pack)
 
-        @pl.loop(0, groups)
+        @pl.loop(0, groups, unroll=2)
         def _(g):
             finish_group(layer, g)
 
@@ -570,7 +617,7 @@
         out_copy(g).wait()
 
 
-def main_call(u, weights, near, far, order, columns, stack, rtab, ctab, mix, bias, sizes, cells):
+def main_call(u, weights, near, far, rtab, ctab, mix, bias, sizes, cells):
     channels, local_rows, cols = u.shape
     layers = weights.shape[0]
     devices = sizes[0] * sizes[1]
@@ -589,12 +636,12 @@
     scratch = pltpu.VMEM
     return pl.pallas_call(
         functools.partial(
-            main_kernel, sizes=sizes, cells=cells, first_part=8,
+            main_kernel, sizes=sizes, cells=cells, first_part=5,
             batch=4 if channels % 4 == 0 else 1,
         ),
         name="operator",
         out_shape=jax.ShapeDtypeStruct((groups * 2 * half, cols), bf16),
-        in_specs=[anywhere] + [vmem] * 10,
+        in_specs=[anywhere] + [vmem] * 7,
         out_specs=anywhere,
         scratch_shapes=[
             scratch((channels, local_rows, cols), bf16),
@@ -627,6 +674,9 @@
             scratch((layers, half, LANES), f32),
             scratch((2 * LANES, cols), jnp.int32),
             scratch((2 * channels, LANES), f32),
+            scratch((2 * half, 2 * half), bf16),
+            scratch((cols, cols), bf16),
+            scratch((layers * half, 8 * layers * channels), bf16),
             dma((groups,)),
             dma((groups,)),
             dma((layers, 8)),
@@ -639,7 +689,7 @@
         compiler_params=pltpu.CompilerParams(
             collective_id=0, has_side_effects=True, vmem_limit_bytes=62 * 1024 * 1024
         ),
-    )(u, weights, near, far, order, columns, stack, rtab, ctab, mix, bias)
+    )(u, weights, near, far, rtab, ctab, mix, bias)
 
 
 def solution(mesh):
@@ -657,51 +707,36 @@
         groups = local_rows // GROUP
         planes = local_cols // LANES
         assert share * per_share in (16, 32, 128)
-        assert groups * GROUP == local_rows and 8 * groups <= LANES
+        assert groups * GROUP == local_rows and 8 * groups <= LANES and groups >= 4
+        assert cells_x % 4 == 0 and cells_y % 4 == 0
         assert planes * LANES == local_cols and planes in (1, 2, 4)
-
-        def group_order(inner):
-            return inner % 8 // 2 * 4 + inner % 2 * 2 + inner // 8
 
         mode = jnp.arange(2 * modes_x, dtype=jnp.int32)
         slot = mode % modes_x % blocks * per_share + mode % modes_x // blocks
         row_mode = jnp.where(slot < modes_x // 2, slot, slot + (cells_x - modes_x))
+        turn = jnp.where(mode < modes_x, 0, 3 * cells_x // 4)
         index = jnp.arange(local_rows, dtype=jnp.int32)
         row_at = index // GROUP * GROUP + group_order(index % GROUP)
         row_at = row_at + lax.axis_index("gx") * local_rows
-        phase = (row_mode[:, None] * row_at[None, :] % cells_x).astype(f32) * (full_turn / cells_x)
-        rtab = jnp.where(mode[:, None] < modes_x, jnp.cos(phase), jnp.sin(phase))
+        phase = (row_mode[:, None] * row_at[None, :] + turn[:, None]) % cells_x
+        rtab = jnp.cos(phase.astype(f32) * (full_turn / cells_x))
 
         index = jnp.arange(local_cols, dtype=jnp.int32)
-        spot = index % LANES * planes + index // LANES
-        col_at = lax.axis_index("gy") * local_cols + spot
-        lane = jnp.arange(LANES, dtype=jnp.int32)[None, :]
-        phase = (col_at[:, None] * (lane % MODES_Y) % cells_y).astype(f32) * (full_turn / cells_y)
-        cosine, sine = jnp.cos(phase), jnp.sin(phase)
-        kind = lane // MODES_Y
-        ctab = jnp.where(kind == 0, cosine, jnp.where(kind == 3, -cosine, -sine))
-
-        at = jnp.arange(GROUP * channels, dtype=jnp.int32)
-        natural = at % channels * GROUP + group_order(at // channels)
-        order = (natural[:, None] == at[None, :]).astype(bf16)
-        back = (natural[None, :] == at[:, None]).astype(bf16)
-        columns = (index[:, None] == spot[None, :]).astype(bf16)
-        columns_back = (index[None, :] == spot[:, None]).astype(bf16)
-        count = 8 * channels
-        at = jnp.arange(layers * count, dtype=jnp.int32)
-        wanted = at % count // channels * (layers * channels)
-        wanted = wanted + at % channels * layers + at // count
-        stack = (wanted[:, None] == at[None, :]).astype(bf16)
+        col_at = lax.axis_index("gy") * local_cols + natural_column(index, local_cols)
+        lane = jnp.arange(LANES, dtype=jnp.int32)
+        turn = jnp.where(lane < MODES_Y, 0, jnp.where(lane < 3 * MODES_Y, 1, 2)) * (cells_y // 4)
+        phase = (col_at[:, None] * (lane % MODES_Y)[None, :] + turn[None, :]) % cells_y
+        ctab = jnp.cos(phase.astype(f32) * (full_turn / cells_y))
 
         field = main_call(
             grid_field[0],
             spectral_weight.transpose(0, 2, 3, 1, 4),
             conv_near.transpose(1, 0, 2),
             conv_far.transpose(1, 0, 2),
-            order, columns, stack, rtab, ctab, mix_logits, channel_bias,
+            rtab, ctab, mix_logits, channel_bias,
             sizes, cells_x * cells_y,
         )
-        return restore_call(field, back, columns_back, channels)[None]
+        return restore_call(field, channels)[None]
 
     in_specs = (
         P(None, None, "gx", "gy"),

time: 126 us -> 109 us (0.87); the launches traced: 126 us -> 108 us
  Pallas kernels: 121 us -> 105 us
  other arithmetic: 5.41 us -> 2.99 us
    pallas_call x1, Pallas kernels: 105 us -> 94.1 us  [main_call(): pl.pallas_call(functools.partial(main_kernel, sizes=sizes, cells=cells, f...]
    pallas_call x1, Pallas kernels: 15.5 us -> 10.6 us  [restore_call(): pl.pallas_call(functools.partial(restore_kernel, chunk=chunk), grid=(grou...]
    select_n x2 -> x0, other arithmetic: 3.16 us -> none  [the longest x1 1.91 us: on_device(): ctab = jnp.where(kind == 0, cosine, jnp.where(kind == 3, -cosine, -sine))]
    cos x0 -> x2, other arithmetic: none -> 2.95 us  [the longest x1 1.74 us: on_device(): ctab = jnp.cos(phase.astype(f32) * (full_turn / cells_y))]
    convert_element_type x2 -> x0, other arithmetic: 2.15 us -> none  [the longest x1 1.12 us: on_device(): columns_back = (index[None, :] == spot[:, None]).astype(bf16)]
where the time goes in v2:
time: 109 us; the launch traced here: 108 us
  Pallas kernels  105 us (96%)
  other arithmetic  2.99 us (3%)
    pallas_call x1, Pallas kernels, main_call(): pl.pallas_call(functools.partial(main_kernel, sizes=sizes, cells=cells, f...  94.1 us
    pallas_call x1, Pallas kernels, restore_call(): pl.pallas_call(functools.partial(restore_kernel, chunk=chunk), grid=(grou...  10.6 us

profile of v2, /device:TPU:1, one launch (start us, length us, event | category | flops | bytes accessed | tf_op | source)
XLA Modules:
  0.0 107.7 jit_solution(12419896068615440371)
XLA Ops:
  0.1 1.2 %fusion.7.rtab_ref = f32[128,256]{1,0:T(8,128)} fusion(s32[128]{0:T(128)S(1)} %get-tuple-element.6, s32[256]{0:T(256)S(1)} %fusion.23, s32[128]{0:T(128)S(1)} %get-tuple-element.5), kind=kLoop, calls=%fused_computation.13 | loop fusion | flops 491520 | bytes 133120 | tf_op jit(solution)/shard_map/cos | solution.py:722
  1.3 1.7 %fusion.3.ctab_ref = f32[512,128]{1,0:T(8,128)} fusion(s32[128]{0:T(128)S(1)} %get-tuple-element.8, s32[128]{0:T(128)S(1)} %get-tuple-element.7, s32[512]{0:T(512)S(1)} %fusion.13), kind=kLoop, calls=%fused_computation.6 | loop fusion | flops 983040 | bytes 265216 | tf_op jit(solution)/shard_map/cos | solution.py:729
  3.0 94.1 %operator.1.value_ref = bf16[5120,512]{1,0:T(8,128)(2,1)} custom-call(bf16[20,256,512]{2,1,0:T(8,128)(2,1)} %bitcast.5, f32[2,20,20,2,64]{4,3,2,1,0:T(2,128)} %bitcast.6, bf16[20,2,180]{2,1,0:T(2,128)(2,1)} %bitcast.8, bf16[20,2,500]{2,1,0:T(2,128)(2,1)} %bitcast.7, f32[128,256]{1,0:T(8,128)} %fusion.7.rtab_ref, f32[512,128]{1,0:T(8,128)} %fusion.3.ctab_ref, ...), custom_call_target="tpu_custom_call" | custom-call | tf_op jit(solution)/shard_map/operator/pallas_call | solution.py:637
  97.1 10.6 %restore.1 = bf16[20,256,512]{2,1,0:T(8,128)(2,1)} custom-call(bf16[5120,512]{1,0:T(8,128)(2,1)} %operator.1.value_ref), custom_call_target="tpu_custom_call" | custom-call | tf_op jit(solution)/shard_map/restore/pallas_call | solution.py:72
  (4 shorter events, 0.0 us)

commit v3 on v2

--- a/solution.py
+++ b/solution.py
@@ -47,21 +47,18 @@
     return jnp.where(left == right, 1.0, 0.0).astype(bf16)
 
 
-def restore_kernel(value_ref, out_ref, back, columns, *, chunk):
+def restore_kernel(value_ref, out_ref, columns, *, chunk):
     channels, _, cols = out_ref.shape
     whole = channels * GROUP
 
     @pl.when(pl.program_id(0) == 0)
     def _():
-        at = natural_order(iota((8, whole), 1), channels)[:1]
-        back[...] = matches(iota((whole, whole), 0), at)
         at = natural_column(iota((cols, LANES), 0), cols)[:, :1]
         columns[...] = matches(at, iota((cols, cols), 1))
 
     for i in range(chunk):
         value = value_ref[i * whole : (i + 1) * whole, :]
         value = jnp.dot(value, columns[...], preferred_element_type=f32).astype(bf16)
-        value = jnp.dot(back[...], value, preferred_element_type=f32).astype(bf16)
         out_ref[:, i * GROUP : (i + 1) * GROUP, :] = value.reshape(channels, GROUP, cols)
 
 
@@ -76,7 +73,7 @@
         in_specs=[pl.BlockSpec((chunk * whole, cols), lambda i: (i, 0))],
         out_specs=pl.BlockSpec((channels, chunk * GROUP, cols), lambda i: (0, i, 0)),
         out_shape=jax.ShapeDtypeStruct((channels, groups * GROUP, cols), bf16),
-        scratch_shapes=[pltpu.VMEM((whole, whole), bf16), pltpu.VMEM((cols, cols), bf16)],
+        scratch_shapes=[pltpu.VMEM((cols, cols), bf16)],
     )(value)
 
 
@@ -85,7 +82,7 @@
     mix_ref, bias_ref, out_ref,
     ubuf, obuf, nst, fst, conv, lhs, lines, carry, pack, packs, edges, hcol, hrow, hcorner,
     sendbuf, recv, mixed, gath, nw, fw, taps, tall, ftab, itab, fwd, inv, mixb, biasb, code, pairs,
-    order, columns, stack,
+    order, back, columns, stack, pick,
     u_sem, out_sem, halo_send, halo_recv, a2a_send, a2a_recv, gat_send, gat_recv,
     *, sizes, cells, first_part, batch,
 ):
@@ -131,6 +128,8 @@
 
     at = natural_order(iota((whole, LANES), 0), channels)[:, :1]
     order[...] = matches(at, iota((whole, whole), 1))
+    at = natural_order(iota((8, whole), 1), channels)[:1]
+    back[...] = matches(iota((whole, whole), 0), at)
     at = natural_column(iota((8, cols), 1), cols)[:1]
     columns[...] = matches(iota((cols, cols), 0), at)
     at = iota((layers * half, LANES), 0)
@@ -171,8 +170,16 @@
         jnp.where((at >= LANES) & (lane < edge), at - LANES - after, -1),
     )
 
-    def edge_pick(k):
-        return jnp.where(code[...] == HALO * k, 1.0, 0.0).astype(bf16)
+    pick[...] = matches(code[...], 0)
+
+    def roll_halves(value, amount):
+        return jnp.concatenate(
+            [pltpu.roll(value[:, i * LANES : (i + 1) * LANES], amount, 1) for i in range(2)], axis=1
+        )
+
+    def edge_columns(packed, k):
+        turned_back = roll_halves(packed, (LANES - HALO * k) % LANES).astype(bf16)
+        return jnp.dot(turned_back, pick[...], preferred_element_type=f32)
 
     depth = 6 * pair
     wide = (depth + LANES - 1) // LANES * LANES
@@ -194,52 +201,53 @@
         for layer in range(layers):
             out_ref[layer] = jnp.concatenate([piece[layer] for piece in pieces], axis=1)
 
-    source = tap_rows(far_ref)
-    count = far_ref.shape[2]
-    target = iota((count, wide), 1)
-    base = jnp.where(
-        target < 5 * channels,
-        target // channels * (5 * channels) + target % channels,
-        -count,
-    )
-    base = iota((count, wide), 0) - base
-    pieces = []
-    for column in range(5):
-        pick = jnp.where(base == column * channels, 1.0, 0.0).astype(bf16)
-        block = jnp.dot(source, pick, preferred_element_type=f32)
-        for row in range(8):
-            tall[rows_of * row : rows_of * (row + 1), :] = (
-                pltpu.roll(block, channels * row, 1) if row else block
-            )
-        pieces.append(spread(fw, column))
-    emit(fw, pieces)
-
-    source = tap_rows(near_ref)
-    count = near_ref.shape[2]
-    target = iota((count, wide), 1)
-    spot, channel = target // channels, target % channels
-    where_row = {-1: 1, 0: 2, 1: 4, 2: 3, 3: 5, 4: 6}
-    bases = []
-    for row in range(4):
-        tap = jnp.full(target.shape, -count, jnp.int32)
-        for step in range(3):
-            tap = jnp.where(
-                spot == where_row[row + step - 1], step * 3 * channels + channel, tap
-            )
-        bases.append(iota((count, wide), 0) - tap)
-    pieces = []
-    for column in range(3):
+    def spread_taps():
+        source = tap_rows(far_ref)
+        count = far_ref.shape[2]
+        target = iota((count, wide), 1)
+        base = jnp.where(
+            target < 5 * channels,
+            target // channels * (5 * channels) + target % channels,
+            -count,
+        )
+        base = iota((count, wide), 0) - base
+        pieces = []
+        for column in range(5):
+            chosen = matches(base, column * channels)
+            block = jnp.dot(source, chosen, preferred_element_type=f32)
+            for row in range(8):
+                tall[rows_of * row : rows_of * (row + 1), :] = (
+                    pltpu.roll(block, channels * row, 1) if row else block
+                )
+            pieces.append(spread(fw, column))
+        emit(fw, pieces)
+
+        source = tap_rows(near_ref)
+        count = near_ref.shape[2]
+        target = iota((count, wide), 1)
+        spot, channel = target // channels, target % channels
+        where_row = {-1: 1, 0: 2, 1: 4, 2: 3, 3: 5, 4: 6}
+        bases = []
         for row in range(4):
-            pick = jnp.where(bases[row] == column * channels, 1.0, 0.0).astype(bf16)
-            block = jnp.dot(source, pick, preferred_element_type=f32)
-            for quad in range(2):
-                full_row = 4 * quad + row
-                index = full_row % 2 * 4 + full_row // 2
-                tall[rows_of * index : rows_of * (index + 1), :] = (
-                    pltpu.roll(block, 4 * channels, 1) if quad else block
+            tap = jnp.full(target.shape, -count, jnp.int32)
+            for step in range(3):
+                tap = jnp.where(
+                    spot == where_row[row + step - 1], step * 3 * channels + channel, tap
                 )
-        pieces.append(spread(nw, column))
-    emit(nw, pieces)
+            bases.append(iota((count, wide), 0) - tap)
+        pieces = []
+        for column in range(3):
+            for row in range(4):
+                chosen = matches(bases[row], column * channels)
+                block = jnp.dot(source, chosen, preferred_element_type=f32)
+                for quad in range(2):
+                    full_row = 4 * quad + row
+                    index = full_row % 2 * 4 + full_row // 2
+                    tall[rows_of * index : rows_of * (index + 1), :] = (
+                        pltpu.roll(block, 4 * channels, 1) if quad else block
+                    )
+            pieces.append(spread(nw, column))
+        emit(nw, pieces)
 
     def near_edges(value):
         low_lanes = iota((value.shape[0], LANES), 1) < LANES // 2
@@ -266,7 +274,7 @@
         carry[0, :, at] = q[3][0]
         carry[1, :, at] = q[3][1]
 
-    def ingest(g, value, layer):
+    def ingest(g, value):
         full = value.astype(f32)
         even, odd = full[:half], full[half:]
         store_rows(g, even, odd, 0)
@@ -275,34 +283,33 @@
         )
         total = pack[...]
         for p in range(2):
-            total = total + lax.dot_general(
+            found = lax.dot_general(
                 value[p * half : (p + 1) * half],
-                edge_pick(2 * g + p),
+                pick[...],
                 (((1,), (1,)), ((), ())),
                 preferred_element_type=f32,
             )
+            total = total + roll_halves(found, HALO * (2 * g + p))
         pack[...] = total
-
-        @pl.when(g == 0)
-        def _():
-            edges[layer, 0] = jnp.concatenate([even[:pair], odd[:pair]], axis=0).astype(bf16)
-
-        @pl.when(g == groups - 1)
-        def _():
-            edges[layer, 1] = jnp.concatenate(
-                [even[3 * pair :], odd[3 * pair :]], axis=0
-            ).astype(bf16)
 
     carry[...] = jnp.zeros_like(carry)
     pack[...] = jnp.zeros_like(pack)
 
-    @pl.loop(0, groups, unroll=2)
-    def _(g):
-        u_copy(g).wait()
-        slab = ubuf[:, pl.ds(pl.multiple_of(g * GROUP, GROUP), GROUP), :].reshape(whole, cols)
-        value = jnp.dot(order[...], slab, preferred_element_type=f32).astype(bf16)
-        value = jnp.dot(value, columns[...], preferred_element_type=f32).astype(bf16)
-        ingest(g, value, 0)
+    @pl.loop(0, groups // 2)
+    def _(b):
+        values = []
+        for i in range(2):
+            u_copy(2 * b + i).wait()
+        for i in range(2):
+            at = pl.ds(pl.multiple_of((2 * b + i) * GROUP, GROUP), GROUP)
+            slab = ubuf[:, at, :].reshape(whole, cols)
+            values.append(jnp.dot(order[...], slab, preferred_element_type=f32).astype(bf16))
+        values = [
+            jnp.dot(value, columns[...], preferred_element_type=f32).astype(bf16)
+            for value in values
+        ]
+        for i in range(2):
+            ingest(2 * b + i, values[i])
 
     pl.semaphore_wait(barrier, devices - 1)
 
@@ -364,7 +371,7 @@
         return jnp.concatenate([high, low, high], axis=0)
 
     def row_transform(layer):
-        @pl.loop(0, channels // batch)
+        @pl.loop(0, channels // batch, unroll=5 if channels // batch % 5 == 0 else 1)
         def _(b):
             parts = [
                 triple(lines[pl.ds(b * batch + i, local_rows, stride=channels), :])
@@ -426,7 +433,7 @@
         def _(k):
             gather_copy(layer, k).wait_recv()
 
-        @pl.loop(0, channels // batch)
+        @pl.loop(0, channels // batch, unroll=5 if channels // batch % 5 == 0 else 1)
         def _(b):
             parts = []
             for i in range(batch):
@@ -448,10 +455,10 @@
                     :, i * LANES : (i + 1) * LANES
                 ]
 
-    def conv_group(layer, g):
+    def conv_groups(layer, g, count):
         def window(rows, shifts, beside):
             own = [rows[:, s * LANES : (s + 1) * LANES] for s in range(planes)]
-            at = iota((depth, LANES), 1)
+            at = iota((rows.shape[0], LANES), 1)
             known = {}
 
             def piece(s, d):
@@ -468,57 +475,73 @@
                     known[plane, move] = value
                 return known[plane, move]
 
-            return jnp.concatenate(
-                [
-                    jnp.concatenate([piece(s, d) for s in range(planes)], axis=1)
-                    for d in shifts
-                ],
-                axis=0,
+            return [jnp.concatenate([piece(s, d) for s in range(planes)], axis=1) for d in shifts]
+
+        rows = nst[pl.ds(pl.multiple_of(g * whole, whole), (2 * count - 1) * half + depth), :]
+        near_columns = window(rows, NEAR, lambda plane: rows[:, cols:])
+        far_columns = []
+        for p in range(2):
+            rows = fst[p, pl.ds(pl.multiple_of(g * half, half), (count - 1) * half + depth), :]
+            far_columns.append(
+                window(rows, FAR, lambda s: rows[:, cols + s * LANES : cols + (s + 1) * LANES])
             )
-
-        near = []
-        for h in range(2):
-            rows = nst[pl.ds(pl.multiple_of(g * whole, whole) + h * half, depth), :]
-            columns = window(rows, NEAR, lambda plane: rows[:, cols:])
-            near.append(jnp.dot(nw[layer], columns, preferred_element_type=f32))
-        parts = []
         bias = jnp.concatenate([biasb[layer]] * planes, axis=1)
-        for p in range(2):
-            rows = fst[p, pl.ds(pl.multiple_of(g * half, half), depth), :]
-            columns = window(
-                rows, FAR, lambda s: rows[:, cols + s * LANES : cols + (s + 1) * LANES]
+
+        def apply(weights, parts, start):
+            columns = jnp.concatenate([part[start : start + depth] for part in parts], axis=0)
+            return jnp.dot(weights, columns, preferred_element_type=f32)
+
+        for i in range(count):
+            near = [apply(nw[layer], near_columns, (2 * i + h) * half) for h in range(2)]
+            parts = []
+            for p in range(2):
+                far = apply(fw[layer], far_columns[p], i * half)
+                side = slice(p * 2 * pair, (p + 1) * 2 * pair)
+                close = jnp.concatenate([near[0][side], near[1][side]], axis=0)
+                total = (
+                    mixb[3 * layer + 1 : 3 * layer + 2, :] * close
+                    + mixb[3 * layer + 2 : 3 * layer + 3, :] * far
+                    + bias
+                )
+                parts.append(total)
+            conv[pl.ds(pl.multiple_of((g + i) * whole, whole), whole), :] = jnp.concatenate(
+                parts, axis=0
             )
-            far = jnp.dot(fw[layer], columns, preferred_element_type=f32)
-            side = slice(p * 2 * pair, (p + 1) * 2 * pair)
-            close = jnp.concatenate([near[0][side], near[1][side]], axis=0)
-            total = (
-                mixb[3 * layer + 1 : 3 * layer + 2, :] * close
-                + mixb[3 * layer + 2 : 3 * layer + 3, :] * far
-                + bias
-            )
-            parts.append(total)
-        conv[pl.ds(pl.multiple_of(g * whole, whole), whole), :] = jnp.concatenate(parts, axis=0)
 
     def out_copy(g):
         rows = pl.ds(pl.multiple_of(g * whole, whole), whole)
         return pltpu.make_async_copy(obuf.at[rows], out_ref.at[rows], out_sem.at[g])
 
-    def finish_group(layer, g):
-        at = pl.ds(pl.multiple_of(g * whole, whole), whole)
-        high, low = split_bf16(lhs[at, :per_device])
-        spectral = jnp.dot(
-            jnp.concatenate([high, low, high], axis=1), inv[...], preferred_element_type=f32
-        )
-        value = conv[at, :] + spectral
-        value = (value * 0.5 * (1.0 + lax.erf(value * (0.5**0.5)))).astype(bf16)
+    def finish_pair(layer, b):
+        spots = [pl.ds(pl.multiple_of((2 * b + i) * whole, whole), whole) for i in range(2)]
+        values = []
+        for at in spots:
+            high, low = split_bf16(lhs[at, :per_device])
+            spectral = jnp.dot(
+                jnp.concatenate([high, low, high], axis=1), inv[...], preferred_element_type=f32
+            )
+            value = conv[at, :] + spectral
+            value = value * 0.5 * (1.0 + lax.erf(value * (0.5**0.5)))
+            values.append(value.astype(bf16))
         if layer + 1 < layers:
-            ingest(g, value, layer + 1)
+            for i in range(2):
+                ingest(2 * b + i, values[i])
         else:
-            obuf[at, :] = value
-            out_copy(g).start()
+            values = [
+                jnp.dot(back[...], value, preferred_element_type=f32).astype(bf16)
+                for value in values
+            ]
+            for i in range(2):
+                obuf[spots[i], :] = values[i]
+            for i in range(2):
+                out_copy(2 * b + i).start()
 
     for layer in range(layers):
         packs[layer] = pack[...].astype(bf16)
+        tops = [fst[p, : 2 * pair, :cols].astype(f32)[pair:] for p in range(2)]
+        edges[layer, 0] = jnp.concatenate(tops, axis=0).astype(bf16)
+        bottoms = [carry[p, :, :cols] for p in range(2)]
+        edges[layer, 1] = jnp.concatenate(bottoms, axis=0).astype(bf16)
         halos = halo_copies(layer)
         for copy in halos:
             copy.start()
@@ -528,30 +551,30 @@
         def _(k):
             a2a_copy(layer, k).start()
 
+        if layer == 0:
+            spread_taps()
         for copy in halos[:2]:
             copy.wait_recv()
         carry[:, :, cols:] = jnp.zeros((2, pair, cols), f32)
+        pack[...] = hcol[layer].astype(f32)
 
         @pl.loop(0, groups, unroll=2)
         def _(g):
-            beside = hcol[layer]
-            parts = [
-                jnp.dot(beside, edge_pick(2 * g + p), preferred_element_type=f32)
-                for p in range(2)
-            ]
+            parts = [edge_columns(pack[...], 2 * g + p) for p in range(2)]
             store_rows(g, parts[0], parts[1], 1)
 
-        cut = 1 + first_part * (groups - 2) // 14
-
-        @pl.loop(1, cut)
-        def _(g):
-            conv_group(layer, g)
+        twos = (groups - 2) // 2
+        cut = first_part * twos // 14
+
+        @pl.loop(0, cut)
+        def _(b):
+            conv_groups(layer, 1 + 2 * b, 2)
 
         mix_modes(layer)
 
-        @pl.loop(cut, groups - 1)
-        def _(g):
-            conv_group(layer, g)
+        @pl.loop(cut, twos)
+        def _(b):
+            conv_groups(layer, 1 + 2 * b, 2)
 
         for copy in halos[2:]:
             copy.wait_recv()
@@ -561,9 +584,7 @@
             main = hrow[layer, side].astype(f32)
             out = []
             for p in range(2):
-                corner = jnp.dot(
-                    hcorner[layer, side], edge_pick(k + p), preferred_element_type=f32
-                )
+                corner = edge_columns(hcorner[layer, side].astype(f32), k + p)
                 corner = corner[:pair] if side else corner[trim - pair :]
                 out.append((main[p * pair : (p + 1) * pair], corner))
             return out
@@ -594,15 +615,15 @@
 
         @pl.loop(0, 2)
         def _(i):
-            conv_group(layer, i * (groups - 1))
+            conv_groups(layer, i * (groups - 1), 1)
 
         inverse_rows(layer)
         carry[...] = jnp.zeros_like(carry)
         pack[...] = jnp.zeros_like(pack)
 
-        @pl.loop(0, groups, unroll=2)
-        def _(g):
-            finish_group(layer, g)
+        @pl.loop(0, groups // 2)
+        def _(b):
+            finish_pair(layer, b)
 
         for copy in halos:
             copy.wait_send()
@@ -636,7 +657,7 @@
     scratch = pltpu.VMEM
     return pl.pallas_call(
         functools.partial(
-            main_kernel, sizes=sizes, cells=cells, first_part=5,
+            main_kernel, sizes=sizes, cells=cells, first_part=6,
             batch=4 if channels % 4 == 0 else 1,
         ),
         name="operator",
@@ -675,8 +696,10 @@
             scratch((2 * LANES, cols), jnp.int32),
             scratch((2 * channels, LANES), f32),
             scratch((2 * half, 2 * half), bf16),
+            scratch((2 * half, 2 * half), bf16),
             scratch((cols, cols), bf16),
             scratch((layers * half, 8 * layers * channels), bf16),
+            scratch((2 * LANES, cols), bf16),
             dma((groups,)),
             dma((groups,)),
             dma((layers, 8)),
@@ -708,6 +731,7 @@
         planes = local_cols // LANES
         assert share * per_share in (16, 32, 128)
         assert groups * GROUP == local_rows and 8 * groups <= LANES and groups >= 4
+        assert groups % 2 == 0
         assert cells_x % 4 == 0 and cells_y % 4 == 0
         assert planes * LANES == local_cols and planes in (1, 2, 4)
 

time: 109 us -> 97.4 us (0.89)
  Pallas kernels: 105 us -> 92.9 us
    pallas_call x1, Pallas kernels: 94.1 us -> 85.9 us  [main_call(): pl.pallas_call(functools.partial(main_kernel, sizes=sizes, cells=cells, f...]
    pallas_call x1, Pallas kernels: 10.6 us -> 6.97 us  [restore_call(): pl.pallas_call(functools.partial(restore_kernel, chunk=chunk), grid=(grou...]
where the time goes in v3:
time: 97.4 us; the launch traced here: 95.9 us
  Pallas kernels  92.9 us (95%)
  other arithmetic  2.99 us (3%)
    pallas_call x1, Pallas kernels, main_call(): pl.pallas_call(functools.partial(main_kernel, sizes=sizes, cells=cells, f...  85.9 us
    pallas_call x1, Pallas kernels, restore_call(): pl.pallas_call(functools.partial(restore_kernel, chunk=chunk), grid=(grou...  6.97 us

profile of v3, /device:TPU:1, one launch (start us, length us, event | category | flops | bytes accessed | tf_op | source)
XLA Modules:
  0.0 95.9 jit_solution(10001696462542347726)
XLA Ops:
  0.1 1.2 %fusion.7.rtab_ref = f32[128,256]{1,0:T(8,128)} fusion(s32[128]{0:T(128)S(1)} %get-tuple-element.6, s32[256]{0:T(256)S(1)} %fusion.23, s32[128]{0:T(128)S(1)} %get-tuple-element.5), kind=kLoop, calls=%fused_computation.13 | loop fusion | flops 491520 | bytes 133120 | tf_op jit(solution)/shard_map/cos | solution.py:746
  1.3 1.7 %fusion.3.ctab_ref = f32[512,128]{1,0:T(8,128)} fusion(s32[128]{0:T(128)S(1)} %get-tuple-element.8, s32[128]{0:T(128)S(1)} %get-tuple-element.7, s32[512]{0:T(512)S(1)} %fusion.13), kind=kLoop, calls=%fused_computation.6 | loop fusion | flops 983040 | bytes 265216 | tf_op jit(solution)/shard_map/cos | solution.py:753
  3.0 85.9 %operator.1.value_ref = bf16[5120,512]{1,0:T(8,128)(2,1)} custom-call(bf16[20,256,512]{2,1,0:T(8,128)(2,1)} %bitcast.5, f32[2,20,20,2,64]{4,3,2,1,0:T(2,128)} %bitcast.6, bf16[20,2,180]{2,1,0:T(2,128)(2,1)} %bitcast.8, bf16[20,2,500]{2,1,0:T(2,128)(2,1)} %bitcast.7, f32[128,256]{1,0:T(8,128)} %fusion.7.rtab_ref, f32[512,128]{1,0:T(8,128)} %fusion.3.ctab_ref, ...), custom_call_target="tpu_custom_call" | custom-call | tf_op jit(solution)/shard_map/operator/pallas_call | solution.py:658
  88.9 7.0 %restore.1 = bf16[20,256,512]{2,1,0:T(8,128)(2,1)} custom-call(bf16[5120,512]{1,0:T(8,128)(2,1)} %operator.1.value_ref), custom_call_target="tpu_custom_call" | custom-call | tf_op jit(solution)/shard_map/restore/pallas_call | solution.py:69
  (4 shorter events, 0.0 us)

commit v4 on v3

--- a/solution.py
+++ b/solution.py
@@ -112,19 +112,19 @@
 
     barrier = pltpu.get_barrier_semaphore()
 
+    def u_copy(g):
+        rows = pl.ds(pl.multiple_of(g * GROUP, GROUP), GROUP)
+        return pltpu.make_async_copy(u_ref.at[:, rows, :], ubuf.at[:, rows, :], u_sem.at[g])
+
+    @pl.loop(0, groups)
+    def _(g):
+        u_copy(g).start()
+
     @pl.loop(1, devices)
     def _(k):
         pl.semaphore_signal(
             barrier, inc=1, device_id=place((me + k) % devices), device_id_type=MESH
         )
-
-    def u_copy(g):
-        rows = pl.ds(pl.multiple_of(g * GROUP, GROUP), GROUP)
-        return pltpu.make_async_copy(u_ref.at[:, rows, :], ubuf.at[:, rows, :], u_sem.at[g])
-
-    @pl.loop(0, groups)
-    def _(g):
-        u_copy(g).start()
 
     at = natural_order(iota((whole, LANES), 0), channels)[:, :1]
     order[...] = matches(at, iota((whole, whole), 1))
@@ -140,8 +140,9 @@
     ftab[...] = jnp.concatenate([high, high, low], axis=1)
     high, low = split_bf16(rtab_ref[...].T)
     itab[...] = jnp.concatenate([high, high, low], axis=1)
-    fwd[...] = ctab_ref[...].astype(bf16)
-    turned_cols = ctab_ref[...].T[:per_device]
+    turned_cols = ctab_ref[...]
+    cosine, sine = turned_cols[:MODES_Y], turned_cols[MODES_Y:]
+    fwd[...] = jnp.concatenate([cosine, sine, sine, -cosine], axis=0).T.astype(bf16)
     weight = jnp.where(iota((per_device, cols), 0) % MODES_Y == 0, 1.0, 2.0) / cells
     high, low = split_bf16(turned_cols * weight)
     inv[...] = jnp.concatenate([high, high, low], axis=0)
@@ -253,9 +254,16 @@
         low_lanes = iota((value.shape[0], LANES), 1) < LANES // 2
         return jnp.where(low_lanes, value[:, :LANES], value[:, cols - LANES :])
 
-    def store_rows(g, even, odd, side):
+    def store_groups(first, values, side):
         at = slice(side * cols, (side + 1) * cols)
-        old_even, old_odd = carry[0, :, at], carry[1, :, at]
+        old = carry[0, :, at], carry[1, :, at]
+        for i, (even, odd) in enumerate(values):
+            old = store_rows(first + i, even, odd, old, side)
+        carry[0, :, at], carry[1, :, at] = old
+
+    def store_rows(g, even, odd, old, side):
+        at = slice(side * cols, (side + 1) * cols)
+        old_even, old_odd = old
         q = [(even[i * pair : (i + 1) * pair], odd[i * pair : (i + 1) * pair]) for i in range(4)]
         near_rows = [old_odd]
         for i in range(4):
@@ -271,26 +279,27 @@
         row = pl.ds(pl.multiple_of(g * half, half), half)
         fst[0, row, at] = jnp.concatenate([old_even, even[: 3 * pair]], axis=0).astype(bf16)
         fst[1, row, at] = jnp.concatenate([old_odd, odd[: 3 * pair]], axis=0).astype(bf16)
-        carry[0, :, at] = q[3][0]
-        carry[1, :, at] = q[3][1]
-
-    def ingest(g, value):
-        full = value.astype(f32)
-        even, odd = full[:half], full[half:]
-        store_rows(g, even, odd, 0)
-        lines[pl.ds(pl.multiple_of(g * whole, whole), whole), :] = jnp.dot(
-            value, fwd[...], preferred_element_type=f32
-        )
+        return q[3]
+
+    def ingest(first, values):
         total = pack[...]
-        for p in range(2):
-            found = lax.dot_general(
-                value[p * half : (p + 1) * half],
-                pick[...],
-                (((1,), (1,)), ((), ())),
-                preferred_element_type=f32,
-            )
-            total = total + roll_halves(found, HALO * (2 * g + p))
+        sums, parts = [], []
+        for i, value in enumerate(values):
+            sums.append(jnp.dot(value, fwd[...], preferred_element_type=f32))
+            for p in range(2):
+                found = lax.dot_general(
+                    value[p * half : (p + 1) * half],
+                    pick[...],
+                    (((1,), (1,)), ((), ())),
+                    preferred_element_type=f32,
+                )
+                total = total + roll_halves(found, HALO * (2 * (first + i) + p))
+            full = value.astype(f32)
+            parts.append((full[:half], full[half:]))
         pack[...] = total
+        for i, found in enumerate(sums):
+            lines[pl.ds(pl.multiple_of((first + i) * whole, whole), whole), :] = found
+        store_groups(first, parts, 0)
 
     carry[...] = jnp.zeros_like(carry)
     pack[...] = jnp.zeros_like(pack)
@@ -308,8 +317,7 @@
             jnp.dot(value, columns[...], preferred_element_type=f32).astype(bf16)
             for value in values
         ]
-        for i in range(2):
-            ingest(2 * b + i, values[i])
+        ingest(2 * b, values)
 
     pl.semaphore_wait(barrier, devices - 1)
 
@@ -524,8 +532,7 @@
             value = value * 0.5 * (1.0 + lax.erf(value * (0.5**0.5)))
             values.append(value.astype(bf16))
         if layer + 1 < layers:
-            for i in range(2):
-                ingest(2 * b + i, values[i])
+            ingest(2 * b, values)
         else:
             values = [
                 jnp.dot(back[...], value, preferred_element_type=f32).astype(bf16)
@@ -558,10 +565,10 @@
         carry[:, :, cols:] = jnp.zeros((2, pair, cols), f32)
         pack[...] = hcol[layer].astype(f32)
 
-        @pl.loop(0, groups, unroll=2)
-        def _(g):
-            parts = [edge_columns(pack[...], 2 * g + p) for p in range(2)]
-            store_rows(g, parts[0], parts[1], 1)
+        @pl.loop(0, groups // 4)
+        def _(b):
+            parts = [edge_columns(pack[...], 8 * b + i) for i in range(8)]
+            store_groups(4 * b, [(parts[2 * i], parts[2 * i + 1]) for i in range(4)], 1)
 
         twos = (groups - 2) // 2
         cut = first_part * twos // 14
@@ -731,7 +738,7 @@
         planes = local_cols // LANES
         assert share * per_share in (16, 32, 128)
         assert groups * GROUP == local_rows and 8 * groups <= LANES and groups >= 4
-        assert groups % 2 == 0
+        assert groups % 4 == 0
         assert cells_x % 4 == 0 and cells_y % 4 == 0
         assert planes * LANES == local_cols and planes in (1, 2, 4)
 
@@ -747,9 +754,9 @@
 
         index = jnp.arange(local_cols, dtype=jnp.int32)
         col_at = lax.axis_index("gy") * local_cols + natural_column(index, local_cols)
-        lane = jnp.arange(LANES, dtype=jnp.int32)
-        turn = jnp.where(lane < MODES_Y, 0, jnp.where(lane < 3 * MODES_Y, 1, 2)) * (cells_y // 4)
-        phase = (col_at[:, None] * (lane % MODES_Y)[None, :] + turn[None, :]) % cells_y
+        mode = jnp.arange(2 * MODES_Y, dtype=jnp.int32)
+        turn = jnp.where(mode < MODES_Y, 0, cells_y // 4)
+        phase = ((mode % MODES_Y)[:, None] * col_at[None, :] + turn[:, None]) % cells_y
         ctab = jnp.cos(phase.astype(f32) * (full_turn / cells_y))
 
         field = main_call(

time: 97.4 us -> 96 us (0.986)
  no operation moved by 1% of the time
where the time goes in v4:
time: 96 us; the launch traced here: 94.9 us
  Pallas kernels  92.4 us (96%)
  other arithmetic  2.48 us (3%)
    pallas_call x1, Pallas kernels, main_call(): pl.pallas_call(functools.partial(main_kernel, sizes=sizes, cells=cells, f...  85.5 us
    pallas_call x1, Pallas kernels, restore_call(): pl.pallas_call(functools.partial(restore_kernel, chunk=chunk), grid=(grou...  6.97 us

profile of v4, /device:TPU:1, one launch (start us, length us, event | category | flops | bytes accessed | tf_op | source)
XLA Modules:
  0.0 94.9 jit_solution(13217594688714620971)
XLA Ops:
  0.1 1.2 %fusion.7.ctab_ref = f32[64,512]{1,0:T(8,128)} fusion(s32[64]{0:T(128)S(1)} %get-tuple-element.7, s32[512]{0:T(512)S(1)} %fusion.13, s32[64]{0:T(128)S(1)} %get-tuple-element.8), kind=kLoop, calls=%fused_computation.13 | loop fusion | flops 491520 | bytes 133632 | tf_op jit(solution)/shard_map/cos | solution.py:760
  1.3 1.2 %fusion.3.rtab_ref = f32[128,256]{1,0:T(8,128)} fusion(s32[128]{0:T(128)S(1)} %get-tuple-element.6, s32[256]{0:T(256)S(1)} %fusion.23, s32[128]{0:T(128)S(1)} %get-tuple-element.5), kind=kLoop, calls=%fused_computation.9 | loop fusion | flops 491520 | bytes 133120 | tf_op jit(solution)/shard_map/cos | solution.py:753
  2.5 85.5 %operator.1.value_ref = bf16[5120,512]{1,0:T(8,128)(2,1)} custom-call(bf16[20,256,512]{2,1,0:T(8,128)(2,1)} %bitcast.5, f32[2,20,20,2,64]{4,3,2,1,0:T(2,128)} %bitcast.6, bf16[20,2,180]{2,1,0:T(2,128)(2,1)} %bitcast.8, bf16[20,2,500]{2,1,0:T(2,128)(2,1)} %bitcast.7, f32[128,256]{1,0:T(8,128)} %fusion.3.rtab_ref, f32[64,512]{1,0:T(8,128)} %fusion.7.ctab_ref, ...), custom_call_target="tpu_custom_call" | custom-call | tf_op jit(solution)/shard_map/operator/pallas_call | solution.py:665
  88.0 7.0 %restore.1 = bf16[20,256,512]{2,1,0:T(8,128)(2,1)} custom-call(bf16[5120,512]{1,0:T(8,128)(2,1)} %operator.1.value_ref), custom_call_target="tpu_custom_call" | custom-call | tf_op jit(solution)/shard_map/restore/pallas_call | solution.py:69
  (4 shorter events, 0.0 us)

commit v5 on v4

--- a/solution.py
+++ b/solution.py
@@ -304,20 +304,20 @@
     carry[...] = jnp.zeros_like(carry)
     pack[...] = jnp.zeros_like(pack)
 
-    @pl.loop(0, groups // 2)
+    @pl.loop(0, groups // 4)
     def _(b):
         values = []
-        for i in range(2):
-            u_copy(2 * b + i).wait()
-        for i in range(2):
-            at = pl.ds(pl.multiple_of((2 * b + i) * GROUP, GROUP), GROUP)
+        for i in range(4):
+            u_copy(4 * b + i).wait()
+        for i in range(4):
+            at = pl.ds(pl.multiple_of((4 * b + i) * GROUP, GROUP), GROUP)
             slab = ubuf[:, at, :].reshape(whole, cols)
             values.append(jnp.dot(order[...], slab, preferred_element_type=f32).astype(bf16))
         values = [
             jnp.dot(value, columns[...], preferred_element_type=f32).astype(bf16)
             for value in values
         ]
-        ingest(2 * b, values)
+        ingest(4 * b, values)
 
     pl.semaphore_wait(barrier, devices - 1)
 
@@ -520,8 +520,8 @@
         rows = pl.ds(pl.multiple_of(g * whole, whole), whole)
         return pltpu.make_async_copy(obuf.at[rows], out_ref.at[rows], out_sem.at[g])
 
-    def finish_pair(layer, b):
-        spots = [pl.ds(pl.multiple_of((2 * b + i) * whole, whole), whole) for i in range(2)]
+    def finish_groups(layer, b):
+        spots = [pl.ds(pl.multiple_of((4 * b + i) * whole, whole), whole) for i in range(4)]
         values = []
         for at in spots:
             high, low = split_bf16(lhs[at, :per_device])
@@ -532,16 +532,16 @@
             value = value * 0.5 * (1.0 + lax.erf(value * (0.5**0.5)))
             values.append(value.astype(bf16))
         if layer + 1 < layers:
-            ingest(2 * b, values)
+            ingest(4 * b, values)
         else:
             values = [
                 jnp.dot(back[...], value, preferred_element_type=f32).astype(bf16)
                 for value in values
             ]
-            for i in range(2):
+            for i in range(4):
                 obuf[spots[i], :] = values[i]
-            for i in range(2):
-                out_copy(2 * b + i).start()
+            for i in range(4):
+                out_copy(4 * b + i).start()
 
     for layer in range(layers):
         packs[layer] = pack[...].astype(bf16)
@@ -628,9 +628,9 @@
         carry[...] = jnp.zeros_like(carry)
         pack[...] = jnp.zeros_like(pack)
 
-        @pl.loop(0, groups // 2)
+        @pl.loop(0, groups // 4)
         def _(b):
-            finish_pair(layer, b)
+            finish_groups(layer, b)
 
         for copy in halos:
             copy.wait_send()

time: 96 us -> 94 us (0.979)
  Pallas kernels: 92.4 us -> 90.3 us
    pallas_call x1, Pallas kernels: 85.5 us -> 83.4 us  [main_call(): pl.pallas_call(functools.partial(main_kernel, sizes=sizes, cells=cells, f...]
where the time goes in v5:
time: 94 us; the launch traced here: 92.8 us
  Pallas kernels  90.3 us (96%)
  other arithmetic  2.48 us (3%)
    pallas_call x1, Pallas kernels, main_call(): pl.pallas_call(functools.partial(main_kernel, sizes=sizes, cells=cells, f...  83.4 us
    pallas_call x1, Pallas kernels, restore_call(): pl.pallas_call(functools.partial(restore_kernel, chunk=chunk), grid=(grou...  6.97 us

profile of v5, /device:TPU:1, one launch (start us, length us, event | category | flops | bytes accessed | tf_op | source)
XLA Modules:
  0.0 92.8 jit_solution(17542277961651395236)
XLA Ops:
  0.1 1.2 %fusion.7.ctab_ref = f32[64,512]{1,0:T(8,128)} fusion(s32[64]{0:T(128)S(1)} %get-tuple-element.7, s32[512]{0:T(512)S(1)} %fusion.13, s32[64]{0:T(128)S(1)} %get-tuple-element.8), kind=kLoop, calls=%fused_computation.13 | loop fusion | flops 491520 | bytes 133632 | tf_op jit(solution)/shard_map/cos | solution.py:760
  1.3 1.2 %fusion.3.rtab_ref = f32[128,256]{1,0:T(8,128)} fusion(s32[128]{0:T(128)S(1)} %get-tuple-element.6, s32[256]{0:T(256)S(1)} %fusion.23, s32[128]{0:T(128)S(1)} %get-tuple-element.5), kind=kLoop, calls=%fused_computation.9 | loop fusion | flops 491520 | bytes 133120 | tf_op jit(solution)/shard_map/cos | solution.py:753
  2.5 83.4 %operator.1.value_ref = bf16[5120,512]{1,0:T(8,128)(2,1)} custom-call(bf16[20,256,512]{2,1,0:T(8,128)(2,1)} %bitcast.5, f32[2,20,20,2,64]{4,3,2,1,0:T(2,128)} %bitcast.6, bf16[20,2,180]{2,1,0:T(2,128)(2,1)} %bitcast.8, bf16[20,2,500]{2,1,0:T(2,128)(2,1)} %bitcast.7, f32[128,256]{1,0:T(8,128)} %fusion.3.rtab_ref, f32[64,512]{1,0:T(8,128)} %fusion.7.ctab_ref, ...), custom_call_target="tpu_custom_call" | custom-call | tf_op jit(solution)/shard_map/operator/pallas_call | solution.py:665
  85.9 7.0 %restore.1 = bf16[20,256,512]{2,1,0:T(8,128)(2,1)} custom-call(bf16[5120,512]{1,0:T(8,128)(2,1)} %operator.1.value_ref), custom_call_target="tpu_custom_call" | custom-call | tf_op jit(solution)/shard_map/restore/pallas_call | solution.py:69
  (4 shorter events, 0.0 us)
